TPU v7x, 768 devices: a whole 4x8x12 slice. The times are simulated.
768 devices in a mesh: grp: 192 (over z, y_hi, x, core), gy: 4 (over y_lo).
Axes of the slice: x: 4, y: 8 (y_hi: 2, y_lo: 4; y = y_hi * 4 + y_lo), z: 12, core: 2. Of those that a mesh axis runs over, the one named last changes fastest.
Arguments:
- potential_warmth: float32 [24, 3072, 2048], P(None, 'grp', 'gy'), may hold values from -2 to 4
- saltiness_anomaly: float32 [24, 3072, 2048], P(None, 'grp', 'gy'), may hold values from -6 to 6
- seawater_velocity: float32 [2, 3072, 2048], P(None, 'grp', 'gy'), may hold values from -2 to 2
- airflow_surface_forcing: float32 [2, 3072, 2048], P(None, 'grp', 'gy'), may hold values from -3 to 3
- glacial_velocity_sigma: float32 [5, 3072, 2048], P(None, 'grp', 'gy'), may hold values from -3 to 3
- category_coverage: float32 [5, 3072, 2048], P(None, 'grp', 'gy'), may hold values from 0.17 to 0.2
- category_thickness: float32 [5, 3072, 2048], P(None, 'grp', 'gy'), may hold values from 0.2 to 1
- seawater_indicator: int32 [3072, 2048], P('grp', 'gy'), may hold values from 0 to 1
- dynamics_indicator: int32 [3072, 2048], P('grp', 'gy'), may hold values from 0 to 1, as said below
- patch_home_position: int32 [192, 16], P('grp', 'gy'), may hold values from -1 to 3, as said below
Outputs:
- potential_warmth_updated: float32 [24, 3072, 2048], P(None, 'grp', 'gy')
- saltiness_updated: float32 [24, 3072, 2048], P(None, 'grp', 'gy')
- coupled_surface_velocity: float32 [2, 3072, 2048], P(None, 'grp', 'gy')
- glacial_patch_update: float32 [5, 3072, 2048], P(None, 'grp', 'gy')
Inputs may be any that keep to these rules, and one draw needn't show every extreme that they name: For a block with ice, patch_home_position = d + p: it goes to slot p from its tile of the device with the same grp index and gy index d; no two blocks of one tile share a value; the first tile row holds 4 blocks with ice in every draw. `dynamics_indicator`: 1 only at cells with seawater_indicator 1 inside blocks whose patch_home_position is not negative.
All inputs are finite; a program needn't handle non-finite values.
Results may differ from a plain program's by a relative error of at most 0.0003.
Values sent between devices are 32-bit elements; how exact they have to be, the bound alone decides.
No kernel may reach another device: no remote copies, remote signals or barrier semaphores. Data moves between devices by JAX's collectives and lax.ppermute only.
A program may use at most 32 MiB of HBM per device.

v0:
```python
import jax
import jax.numpy as jnp
from jax import lax
from jax.sharding import PartitionSpec as P

NSUB = 4


DIFFUSIVITY = 0.2
STRENGTH_COEF = 20.0
MIN_MASS = 0.5
RELAX_RATE = 0.5
ECCENTRIC = 4.0
DELTA_FLOOR = 0.0025
SPEED_FLOOR = 0.01
CORIOLIS = 0.5
HEAT_COEF = 4.0
THIN_LIMIT = 0.1
FREEZING = -1.8
WARMTH_FACTOR = 0.05
STRESS_SCALE = 0.5


def extended(cells, sides, width):
    for axis, dim in sides:
        count = lax.axis_size(axis)
        head = lax.slice_in_dim(cells, 0, width, axis=dim)
        tail = lax.slice_in_dim(cells, cells.shape[dim] - width, cells.shape[dim], axis=dim)
        cells = jnp.concatenate(
            [
                lax.ppermute(tail, axis, [(i, (i + 1) % count) for i in range(count)]),
                cells,
                lax.ppermute(head, axis, [((i + 1) % count, i) for i in range(count)]),
            ],
            axis=dim,
        )
    return cells


def east_of(field, offset):
    return jnp.roll(field, -offset, axis=-2)


def north_of(field, offset):
    border = jnp.zeros_like(field[..., :1])
    if offset > 0:
        return jnp.concatenate([field[..., 1:], border], axis=-1)
    return jnp.concatenate([border, field[..., :-1]], axis=-1)


def evp_subcycles(
    vel_u,
    vel_v,
    sig_one,
    sig_two,
    sig_shear,
    cur_u,
    cur_v,
    concentration,
    thickness,
    wind_u,
    wind_v,
    glacial_indicator,
):
    strength = thickness * jnp.exp(-STRENGTH_COEF * (1.0 - concentration))
    ice_mass = thickness + MIN_MASS
    for subcycle in range(NSUB):
        u_east = east_of(vel_u, 1) - vel_u
        v_north = north_of(vel_v, 1) - vel_v
        u_north = north_of(vel_u, 1) - vel_u
        v_east = east_of(vel_v, 1) - vel_v
        divergence = u_east + v_north
        tension = u_east - v_north
        shear_rate = u_north + v_east
        deform_rate = jnp.sqrt(
            divergence * divergence
            + (tension * tension + shear_rate * shear_rate) / ECCENTRIC
            + DELTA_FLOOR
        )
        viscous = strength / deform_rate
        sig_one = (
            glacial_indicator
            * (sig_one + RELAX_RATE * (viscous * divergence - strength))
            / (1.0 + RELAX_RATE)
        )
        sig_two = (
            glacial_indicator
            * (sig_two + RELAX_RATE * viscous * tension / ECCENTRIC)
            / (1.0 + RELAX_RATE)
        )
        sig_shear = (
            glacial_indicator
            * (sig_shear + RELAX_RATE * viscous * shear_rate / ECCENTRIC)
            / (1.0 + RELAX_RATE)
        )
        back_one_x = sig_one - east_of(sig_one, -1)
        back_two_x = sig_two - east_of(sig_two, -1)
        back_one_y = sig_one - north_of(sig_one, -1)
        back_two_y = sig_two - north_of(sig_two, -1)
        force_u = 0.5 * (back_one_x + back_two_x) + (sig_shear - north_of(sig_shear, -1))
        force_v = 0.5 * (back_one_y - back_two_y) + (sig_shear - east_of(sig_shear, -1))
        rel_speed = jnp.sqrt((cur_u - vel_u) ** 2 + (cur_v - vel_v) ** 2 + SPEED_FLOOR)
        water_coef = concentration * rel_speed
        implicit = ice_mass + water_coef
        new_u = (
            glacial_indicator
            * (
                ice_mass * vel_u
                + force_u
                + wind_u
                + water_coef * cur_u
                + CORIOLIS * ice_mass * vel_v
            )
            / implicit
        )
        new_v = (
            glacial_indicator
            * (
                ice_mass * vel_v
                + force_v
                + wind_v
                + water_coef * cur_v
                - CORIOLIS * ice_mass * vel_u
            )
            / implicit
        )
        vel_u, vel_v = (new_u, new_v)
    rel_speed = jnp.sqrt((cur_u - vel_u) ** 2 + (cur_v - vel_v) ** 2 + SPEED_FLOOR)
    water_coef = concentration * rel_speed
    stress_u = glacial_indicator * water_coef * (vel_u - cur_u)
    stress_v = glacial_indicator * water_coef * (vel_v - cur_v)
    return ((vel_u, vel_v, sig_one, sig_two, sig_shear), (stress_u, stress_v))


def seabed_exchange(
    surface_temp, category_coverage, category_thickness, glacial_indicator, cat_axis
):
    denominator = category_thickness + THIN_LIMIT * category_coverage
    denominator = jnp.where(denominator > 0.0, denominator, 1.0)
    per_cat = HEAT_COEF * category_coverage * category_coverage / denominator
    return glacial_indicator * (surface_temp - FREEZING) * jnp.sum(per_cat, axis=cat_axis)


def close_rims(padded, width):
    lat_index = lax.axis_index("gy")
    groups = lax.axis_size("gy")
    columns = jnp.arange(padded.shape[-1])
    low_rim = (columns < width) & (lat_index == 0)
    high_rim = (columns >= padded.shape[-1] - width) & (lat_index == groups - 1)
    return jnp.where(low_rim | high_rim, 0.0, padded)


def diffuse_tile(wide):
    fields = wide[:-1]
    wet_wide = wide[-1]
    centre = fields[:, 1:-1, 1:-1]
    inflow = jnp.zeros_like(centre)
    for row_cut, col_cut in (
        (slice(2, None), slice(1, -1)),
        (slice(None, -2), slice(1, -1)),
        (slice(1, -1), slice(2, None)),
        (slice(1, -1), slice(None, -2)),
    ):
        inflow = inflow + wet_wide[row_cut, col_cut] * (fields[:, row_cut, col_cut] - centre)
    return centre + DIFFUSIVITY * wet_wide[1:-1, 1:-1] * inflow


def interior(field):
    return field[..., NSUB : field.shape[-2] - NSUB, NSUB : field.shape[-1] - NSUB]


def run_blocks(windows):
    state, stress = evp_subcycles(*[windows[:, :, plane_number] for plane_number in range(12)])
    owned_state = jnp.stack([interior(member) for member in state], axis=2)
    return (owned_state, [interior(member) for member in stress])


def per_device(
    potential_warmth,
    saltiness_anomaly,
    seawater_velocity,
    airflow_surface_forcing,
    glacial_velocity_sigma,
    category_coverage,
    category_thickness,
    seawater_indicator,
    dynamics_indicator,
    patch_home_position,
):
    vertical_count_value = potential_warmth.shape[0]
    patch_east_count = potential_warmth.shape[1]
    patch_north_count = potential_warmth.shape[2]
    nblock = patch_home_position.shape[1]
    block_len = patch_north_count // nblock
    groups = lax.axis_size("gy")
    pair_count = nblock // groups
    seawater_points = seawater_indicator.astype(jnp.float32)
    glacial_indicator = dynamics_indicator.astype(jnp.float32)
    concentration = jnp.sum(category_coverage, axis=0)
    thickness = jnp.sum(category_thickness, axis=0)
    quantity_stack = jnp.concatenate(
        [potential_warmth, saltiness_anomaly, seawater_points[None]], axis=0
    )
    ice_stack = jnp.concatenate(
        [
            glacial_velocity_sigma,
            seawater_velocity,
            concentration[None],
            thickness[None],
            airflow_surface_forcing,
            glacial_indicator[None],
        ],
        axis=0,
    )
    joined = extended(
        jnp.concatenate([quantity_stack, ice_stack], axis=0), (("grp", 1), ("gy", 2)), NSUB
    )
    joined = close_rims(joined, NSUB)
    rim_start = NSUB - 1
    tracer_wide = joined[
        : 2 * vertical_count_value + 1,
        rim_start : rim_start + patch_east_count + 2,
        rim_start : rim_start + patch_north_count + 2,
    ]
    ice_wide = joined[2 * vertical_count_value + 1 :]
    smoothed_field = diffuse_tile(tracer_wide)
    windows = jnp.stack(
        [
            ice_wide[
                :, :, block_number * block_len : block_number * block_len + block_len + 2 * NSUB
            ]
            for block_number in range(nblock)
        ],
        axis=0,
    )
    chooser = (
        patch_home_position[0][None, :] == jnp.arange(nblock, dtype=jnp.int32)[:, None]
    ).astype(jnp.float32)
    local_state, local_stress = run_blocks(windows[:, None])
    stress_fields = jnp.stack([local_stress[0][:, 0], local_stress[1][:, 0]], axis=1)
    stress_fields = stress_fields.transpose(1, 2, 0, 3).reshape(
        2, patch_east_count, patch_north_count
    )
    picked = jnp.einsum(
        "sb,bfxy->sfxy", chooser, local_state[:, 0], precision=lax.Precision.HIGHEST
    )
    owned_state = lax.all_to_all(
        picked.reshape((groups, pair_count) + picked.shape[1:]),
        "gy",
        split_axis=0,
        concat_axis=0,
        tiled=True,
    )
    heat_exchange = seabed_exchange(
        potential_warmth[0], category_coverage, category_thickness, glacial_indicator, 0
    )
    potential_warmth_updated = smoothed_field[:vertical_count_value]
    potential_warmth_updated = potential_warmth_updated.at[0].add(
        -WARMTH_FACTOR * seawater_points * heat_exchange
    )
    saltiness_updated = smoothed_field[vertical_count_value : 2 * vertical_count_value]
    coupled_surface_velocity = seawater_points * (seawater_velocity + STRESS_SCALE * stress_fields)
    glacial_patch_update = (
        owned_state.reshape(nblock, 5, patch_east_count, block_len)
        .transpose(1, 2, 0, 3)
        .reshape(5, patch_east_count, patch_north_count)
    )
    return (
        potential_warmth_updated,
        saltiness_updated,
        coupled_surface_velocity,
        glacial_patch_update,
    )


def solution(mesh):
    placed = (
        P(None, "grp", "gy"),
        P(None, "grp", "gy"),
        P(None, "grp", "gy"),
        P(None, "grp", "gy"),
        P(None, "grp", "gy"),
        P(None, "grp", "gy"),
        P(None, "grp", "gy"),
        P("grp", "gy"),
        P("grp", "gy"),
        P("grp", "gy"),
    )
    return jax.shard_map(
        per_device,
        mesh=mesh,
        in_specs=placed,
        out_specs=(
            P(None, "grp", "gy"),
            P(None, "grp", "gy"),
            P(None, "grp", "gy"),
            P(None, "grp", "gy"),
        ),
        check_vma=False,
    )
```

profile of v0, /device:TPU:8, one launch (start us, length us, event | category | flops | bytes accessed | tf_op | source)
XLA Modules:
  0.0 80.0 jit_solution(3820522126054677446)
XLA Ops:
  0.7 1.3 %constant_dynamic-update-slice_fusion.4 = f32[61,16,512]{2,1,0:T(8,128)S(1)} fusion(f32[24,16,512]{2,1,0:T(8,128)} %param.12), kind=kLoop, calls=%fused_computation.192 | loop fusion | bytes 1572864
  2.0 0.7 fusion.11
  2.7 0.1 constant_dynamic-update-slice_fusion.3
  2.8 0.1 copy-done.5
  3.0 0.2 fusion.108
  3.2 1.9 %collective-permute-start = (f32[61,4,512]{2,1,0:T(4,128)S(1)}, f32[61,4,512]{2,1,0:T(4,128)S(1)}, u32[]{:S(2)}, u32[]{:S(2)}) collective-permute-start(f32[61,4,512]{2,1,0:T(4,128)S(1)} %get-tuple-element.32), channel_id=1, source_target_pairs={{0,4},{4,8},{8,12},{12,16},{16,20},{20,24},{24,28},{28,32},{32,36}... | collective-permute-start | bytes 1499144 | tf_op jit(solution)/shard_map/ppermute | solution.py:31
  5.1 20.6 %collective-permute-start.1 = (f32[61,4,512]{2,1,0:T(4,128)S(1)}, f32[61,4,512]{2,1,0:T(4,128)}, u32[]{:S(2)}, u32[]{:S(2)}) collective-permute-start(f32[61,4,512]{2,1,0:T(4,128)S(1)} %get-tuple-element.33), channel_id=1, source_target_pairs={{4,0},{8,4},{12,8},{16,12},{20,16},{24,20},{28,24},{32,28},{36,32}... | collective-permute-start | bytes 1499144 | tf_op jit(solution)/shard_map/ppermute | solution.py:33
  25.7 8.3 %collective-permute-done = f32[61,4,512]{2,1,0:T(4,128)S(1)} collective-permute-done((f32[61,4,512]{2,1,0:T(4,128)S(1)}, f32[61,4,512]{2,1,0:T(4,128)S(1)}, u32[]{:S(2)}, u32[]{:S(2)}) %collective-permute-start) | collective-permute-done | bytes 499744 | tf_op jit(solution)/shard_map/ppermute | solution.py:31
  34.1 0.8 copy-done.1
  34.9 1.5 %pad_maximum_fusion.2 = (f32[61,24,4]{2,1,0:T(8,128)S(1)}, f32[61,24,4]{2,1,0:T(8,128)S(1)}) fusion(f32[61,4,512]{2,1,0:T(4,128)} %collective-permute-done.1, f32[61,16,512]{2,1,0:T(8,128)S(1)} %bitcast_dynamic-update-slice_fusion.2, f32[61,4,512]{2,1,0:T(4,128)} %copy-done.1), kind=kLoop, calls=%fused_computation.18 | loop fusion | flops 23424 | bytes 3045120 | tf_op jit(solution)/shard_map/slice | solution.py:28
  36.4 1.0 %copy.25 = f32[61,24,4]{0,1,2:T(8,128)} copy(f32[61,24,4]{2,1,0:T(8,128)S(1)} %get-tuple-element.30) | data formatting | bytes 46848 | tf_op jit(solution)/shard_map/slice | solution.py:28
  37.4 2.0 %collective-permute-start.2 = (f32[61,24,4]{0,1,2:T(8,128)}, f32[61,24,4]{0,1,2:T(8,128)S(1)}, u32[]{:S(2)}, u32[]{:S(2)}) collective-permute-start(f32[61,24,4]{0,1,2:T(8,128)} %copy.25), channel_id=1, source_target_pairs={{0,1},{1,2},{2,3},{3,0},{4,5},{5,6},{6,7},{7,4},{8,9},{9,10},{10,1... | collective-permute-start | bytes 70280 | tf_op jit(solution)/shard_map/ppermute | solution.py:31
  39.4 0.3 copy.26
  39.7 3.8 %collective-permute-start.3 = (f32[61,24,4]{0,1,2:T(8,128)S(1)}, f32[61,24,4]{0,1,2:T(8,128)}, u32[]{:S(2)}, u32[]{:S(2)}) collective-permute-start(f32[61,24,4]{0,1,2:T(8,128)S(1)} %copy.26), channel_id=1, source_target_pairs={{1,0},{2,1},{3,2},{0,3},{5,4},{6,5},{7,6},{4,7},{9,8},{10,9},{11,1... | collective-permute-start | bytes 70280 | tf_op jit(solution)/shard_map/ppermute | solution.py:33
  43.6 0.6 convert_element_type.7
  44.2 0.4 copy.27
  44.6 2.1 %collective-permute-done.3 = f32[61,24,4]{0,1,2:T(8,128)} collective-permute-done((f32[61,24,4]{0,1,2:T(8,128)S(1)}, f32[61,24,4]{0,1,2:T(8,128)}, u32[]{:S(2)}, u32[]{:S(2)}) %collective-permute-start.3) | collective-permute-done | bytes 23456 | tf_op jit(solution)/shard_map/ppermute | solution.py:33
  46.7 1.2 %copy.28 = f32[61,24,4]{2,1,0:T(8,128)S(1)} copy(f32[61,24,4]{0,1,2:T(8,128)} %collective-permute-done.3) | data formatting | bytes 46848 | tf_op jit(solution)/shard_map/ppermute | solution.py:33
  47.9 3.4 %maximum_select_fusion = f32[61,24,520]{2,1,0:T(8,128)S(1)} fusion(f32[61,24,4]{2,1,0:T(8,128)S(1)} %copy.28, f32[61,4,512]{2,1,0:T(4,128)} %collective-permute-done.1, f32[61,16,512]{2,1,0:T(8,128)S(1)} %bitcast_dynamic-update-slice_fusion.2, f32[61,4,512]{2,1,0:T(4,128)} %copy-done.1, f32[61,24,4]{2,1,0:T(8,128)S(1)} %copy.27, pred[520]{0:T(1024)(128)(4,1)S(1)} %fusion.100), kind=kLoop, calls=%fused_computation | loop fusion | flops 3806400 | bytes 6090760 | tf_op jit(solution)/shard_map/jit(_where)/select_n | solution.py:150
  51.3 0.1 slice_bitcast_fusion.2
  51.4 0.3 copy.29
  51.7 0.3 copy.30
  52.0 0.3 copy.31
  52.3 0.2 stack.39
  52.5 1.2 %maximum_bitcast_fusion = f32[4,1,12,24,136]{4,0,3,2,1:T(4,128)S(1)} fusion(f32[1,12,24,136]{3,0,2,1:T(1,128)S(1)} %stack.39, f32[1,12,24,136]{3,0,2,1:T(1,128)S(1)} %copy.31, f32[1,12,24,136]{3,0,2,1:T(1,128)S(1)} %copy.30, f32[1,12,24,136]{3,0,2,1:T(1,128)S(1)} %copy.29), kind=kLoop, calls=%fused_computation.14 | loop fusion | flops 470016 | bytes 1253376 | tf_op jit(solution)/shard_map/broadcast_in_dim | solution.py:239
  53.8 0.1 slice.476
  53.9 0.1 slice.475
  54.1 0.2 fusion.20
  54.3 0.2 fusion.17
  54.5 0.3 fusion.30
  54.8 0.1 slice.496
  55.0 0.3 fusion.37
  55.3 0.1 slice.495
  55.5 0.2 multiply_multiply_fusion.9
  55.7 0.2 multiply_multiply_fusion.10
  55.9 0.3 fusion.47
  56.2 0.1 slice.511
  56.4 0.3 fusion.54
  56.7 0.1 slice.510
  56.9 0.2 multiply_multiply_fusion.7
  57.2 0.2 multiply_multiply_fusion.5
  57.4 0.3 fusion.64
  57.7 0.1 slice.526
  57.8 0.3 fusion.71
  58.2 0.1 slice.525
  58.3 0.2 multiply_multiply_fusion.4
  58.6 0.2 multiply_multiply_fusion.2
  58.8 0.1 slice_bitcast_fusion.15
  58.9 0.6 multiply_multiply_fusion.1
  59.5 0.1 bitcast_dynamic-update-slice_fusion.1
  59.5 0.1 bitcast_dynamic-update-slice_fusion
  59.7 0.1 fusion.93
  59.8 0.1 fusion.92
  59.9 0.1 fusion.91
  60.0 0.3 convolution_bitcast_fusion
  60.2 0.7 copy.32
  60.9 7.5 %all-to-all-start = ((f32[4,1,5,16,128]{4,3,2,1,0:T(8,128)}), f32[4,1,5,16,128]{4,3,2,1,0:T(8,128)S(1)}, u32[]{:S(2)}, u32[]{:S(2)}) async-start(f32[4,1,5,16,128]{4,3,2,1,0:T(8,128)} %copy.32), calls=%async_computation | async-start | bytes 327680 | tf_op jit(solution)/shard_map/all_to_all | solution.py:247
  68.4 0.1 slice_multiply_fusion
  68.5 8.1 %fusion.3 = f32[48,16,512]{2,1,0:T(8,128)S(1)} fusion(f32[61,24,520]{2,1,0:T(8,128)} %copy-done, f32[16,512]{1,0:T(8,128)S(1)} %get-tuple-element.51, f32[16,512]{1,0:T(8,128)S(1)} %get-tuple-element.52, f32[16,512]{1,0:T(8,128)S(1)} %get-tuple-element.53, f32[16,512]{1,0:T(8,128)S(1)} %get-tuple-element.54, f32[16,512]{1,0:T(8,128)S(1)} %get-tuple-element.50), kind=kLoop, calls=%fused_computation.5 | loop fusion | flops 5111808 | bytes 9601024 | tf_op jit(solution)/shard_map/add | solution.py:165
  76.6 1.0 %fusion.109 = (f32[24,16,512]{2,1,0:T(8,128)}, f32[24,16,512]{2,1,0:T(8,128)S(1)}) fusion(f32[48,16,512]{2,1,0:T(8,128)S(1)} %fusion.3), kind=kLoop, calls=%fused_computation.202 | loop fusion | bytes 3145728 | tf_op jit(solution)/shard_map/slice | solution.py:261
  77.6 0.8 fusion.96
  78.4 0.1 fusion.95
  78.7 0.7 add_multiply_fusion
  79.3 0.7 copy_bitcast_fusion
  (84 shorter events, 0.4 us)
Async XLA Ops:
  0.6 1.3 %copy-start.8 = (f32[5,16,512]{2,1,0:T(8,128)S(1)}, f32[5,16,512]{2,1,0:T(8,128)}, u32[]{:S(2)}) copy-start(f32[5,16,512]{2,1,0:T(8,128)} %param.17) | copy-start | bytes 491524
  0.6 1.3 %copy-start.7 = (f32[5,16,512]{2,1,0:T(8,128)S(1)}, f32[5,16,512]{2,1,0:T(8,128)}, u32[]{:S(2)}) copy-start(f32[5,16,512]{2,1,0:T(8,128)} %param.18) | copy-start | bytes 491524
  0.7 2.0 %copy-start.2 = (f32[24,16,512]{2,1,0:T(8,128)S(1)}, f32[24,16,512]{2,1,0:T(8,128)}, u32[]{:S(2)}) copy-start(f32[24,16,512]{2,1,0:T(8,128)} %param.13) | copy-start | bytes 2359300
  0.7 2.1 %copy-start.4 = (s32[16,512]{1,0:T(8,128)S(1)}, s32[16,512]{1,0:T(8,128)}, u32[]{:S(2)}) copy-start(s32[16,512]{1,0:T(8,128)} %param.19) | copy-start | bytes 98308
  0.7 2.1 %copy-start.9 = (f32[5,16,512]{2,1,0:T(8,128)S(1)}, f32[5,16,512]{2,1,0:T(8,128)}, u32[]{:S(2)}) copy-start(f32[5,16,512]{2,1,0:T(8,128)} %param.16) | copy-start | bytes 491524
  2.0 0.9 %copy-start.5 = (f32[2,16,512]{2,1,0:T(8,128)S(1)}, f32[2,16,512]{2,1,0:T(8,128)}, u32[]{:S(2)}) copy-start(f32[2,16,512]{2,1,0:T(8,128)} %param.14) | copy-start | bytes 196612
  2.0 0.9 %copy-start.14 = (f32[2,16,512]{2,1,0:T(8,128)S(1)}, f32[2,16,512]{2,1,0:T(8,128)}, u32[]{:S(2)}) copy-start(f32[2,16,512]{2,1,0:T(8,128)} %param.15) | copy-start | bytes 196612
  2.0 0.9 %copy-start.11 = (s32[16,512]{1,0:T(8,128)S(1)}, s32[16,512]{1,0:T(8,128)}, u32[]{:S(2)}) copy-start(s32[16,512]{1,0:T(8,128)} %param.20) | copy-start | bytes 98308
  3.2 30.9 %collective-permute-start = (f32[61,4,512]{2,1,0:T(4,128)S(1)}, f32[61,4,512]{2,1,0:T(4,128)S(1)}, u32[]{:S(2)}, u32[]{:S(2)}) collective-permute-start(f32[61,4,512]{2,1,0:T(4,128)S(1)} %get-tuple-element.32), channel_id=1, source_target_pairs={{0,4},{4,8},{8,12},{12,16},{16,20},{20,24},{24,28},{28,32},{32,36}... | collective-permute-start | bytes 1499144 | tf_op jit(solution)/shard_map/ppermute | solution.py:31
  5.1 29.7 %collective-permute-start.1 = (f32[61,4,512]{2,1,0:T(4,128)S(1)}, f32[61,4,512]{2,1,0:T(4,128)}, u32[]{:S(2)}, u32[]{:S(2)}) collective-permute-start(f32[61,4,512]{2,1,0:T(4,128)S(1)} %get-tuple-element.33), channel_id=1, source_target_pairs={{4,0},{8,4},{12,8},{16,12},{20,16},{24,20},{28,24},{32,28},{36,32}... | collective-permute-start | bytes 1499144 | tf_op jit(solution)/shard_map/ppermute | solution.py:33
  34.1 0.8 copy-start.1
  37.4 6.8 %collective-permute-start.2 = (f32[61,24,4]{0,1,2:T(8,128)}, f32[61,24,4]{0,1,2:T(8,128)S(1)}, u32[]{:S(2)}, u32[]{:S(2)}) collective-permute-start(f32[61,24,4]{0,1,2:T(8,128)} %copy.25), channel_id=1, source_target_pairs={{0,1},{1,2},{2,3},{3,0},{4,5},{5,6},{6,7},{7,4},{8,9},{9,10},{10,1... | collective-permute-start | bytes 70280 | tf_op jit(solution)/shard_map/ppermute | solution.py:31
  39.7 7.0 %collective-permute-start.3 = (f32[61,24,4]{0,1,2:T(8,128)S(1)}, f32[61,24,4]{0,1,2:T(8,128)}, u32[]{:S(2)}, u32[]{:S(2)}) collective-permute-start(f32[61,24,4]{0,1,2:T(8,128)S(1)} %copy.26), channel_id=1, source_target_pairs={{1,0},{2,1},{3,2},{0,3},{5,4},{6,5},{7,6},{4,7},{9,8},{10,9},{11,1... | collective-permute-start | bytes 70280 | tf_op jit(solution)/shard_map/ppermute | solution.py:33
  51.3 7.5 %copy-start = (f32[61,24,520]{2,1,0:T(8,128)}, f32[61,24,520]{2,1,0:T(8,128)S(1)}, u32[]{:S(2)}) copy-start(f32[61,24,520]{2,1,0:T(8,128)S(1)} %maximum_select_fusion) | copy-start | bytes 9135364
  58.8 1.2 %copy-start.15 = (s32[1,4]{1,0:T(1,128)S(1)}, s32[1,4]{1,0:T(1,128)}, u32[]{:S(2)}) copy-start(s32[1,4]{1,0:T(1,128)} %param.21) | copy-start | bytes 52
  60.9 18.4 %all-to-all-start = ((f32[4,1,5,16,128]{4,3,2,1,0:T(8,128)}), f32[4,1,5,16,128]{4,3,2,1,0:T(8,128)S(1)}, u32[]{:S(2)}, u32[]{:S(2)}) async-start(f32[4,1,5,16,128]{4,3,2,1,0:T(8,128)} %copy.32), calls=%async_computation | async-start | bytes 327680 | tf_op jit(solution)/shard_map/all_to_all | solution.py:247
  76.6 1.1 %copy-start.12 = (s32[16,512]{1,0:T(8,128)S(1)}, s32[16,512]{1,0:T(8,128)}, u32[]{:S(2)}) copy-start(s32[16,512]{1,0:T(8,128)} %param.20) | copy-start | bytes 98308
  76.6 1.1 %copy-start.13 = (f32[16,512]{1,0:T(8,128)S(1)}, f32[16,512]{1,0:T(8,128)}, u32[]{:S(2)}) copy-start(f32[16,512]{1,0:T(8,128)} %get-tuple-element.16) | copy-start | bytes 98308
  76.6 2.1 %copy-start.6 = (f32[2,16,512]{2,1,0:T(8,128)S(1)}, f32[2,16,512]{2,1,0:T(8,128)}, u32[]{:S(2)}) copy-start(f32[2,16,512]{2,1,0:T(8,128)} %param.14) | copy-start | bytes 196612
  76.6 2.1 %copy-start.10 = (f32[16,512]{1,0:T(8,128)S(1)}, f32[16,512]{1,0:T(8,128)}, u32[]{:S(2)}) copy-start(f32[16,512]{1,0:T(8,128)} %convert_element_type.7) | copy-start | bytes 98308
  78.4 1.6 %copy-start.3 = (f32[24,16,512]{2,1,0:T(8,128)}, f32[24,16,512]{2,1,0:T(8,128)S(1)}, u32[]{:S(2)}) copy-start(f32[24,16,512]{2,1,0:T(8,128)S(1)} %fusion.96) | copy-start | bytes 2359300
where the time goes:
time: 80.6 us; the launch traced here: 80 us
  starting transfers between devices  35.8 us (44%)
  other arithmetic  21.4 us (27%)
  local copies, waits for them, and re-layouts  10.6 us (13%)
  waiting for transfers between devices  10.5 us (13%)
  between operations  1.49 us (2%)
    ppermute x2, starting transfers between devices, extended(): lax.ppermute(head, axis, [((i + 1) % count, i) for i in range(count)])  24.4 us
    ppermute x2, waiting for transfers between devices, extended(): lax.ppermute(tail, axis, [(i, (i + 1) % count) for i in range(count)])  8.34 us
    add x1, other arithmetic, diffuse_tile(): return centre + DIFFUSIVITY * wet_wide[1:-1, 1:-1] * inflow  8.08 us
    all_to_all x1, starting transfers between devices, per_device(): lax.all_to_all(picked.reshape((groups, pair_count) + picked.shape[1:]), '...  7.45 us
    ppermute x2, starting transfers between devices, extended(): lax.ppermute(tail, axis, [(i, (i + 1) % count) for i in range(count)])  3.92 us
    select_n x1, other arithmetic, close_rims(): return jnp.where(low_rim | high_rim, 0.0, padded)  3.42 us
    unnamed x43, local copies, waits for them, and re-layouts  2.67 us
    ppermute x2, waiting for transfers between devices, extended(): lax.ppermute(head, axis, [((i + 1) % count, i) for i in range(count)])  2.12 us
  transfers between devices with their start and end apart: 5, of which 2 were waited for; matrix products, arithmetic and copies ran while one was open for 15% of the time, Pallas kernels for 0%

commit v1 on v0

v1 whole, which is shorter than its diff:
```python
import jax
import jax.numpy as jnp
from jax import lax
from jax.experimental import pallas as pl
from jax.experimental.pallas import tpu as pltpu
from jax.sharding import PartitionSpec as P


NSUB = 4
DIFFUSIVITY = 0.2
STRENGTH_COEF = 20.0
MIN_MASS = 0.5
RELAX_RATE = 0.5
ECCENTRIC = 4.0
DELTA_FLOOR = 0.0025
SPEED_FLOOR = 0.01
CORIOLIS = 0.5
HEAT_COEF = 4.0
THIN_LIMIT = 0.1
FREEZING = -1.8
WARMTH_FACTOR = 0.05
STRESS_SCALE = 0.5

U, _, _, _, _, UO, VO, AREA, THICK, WX, WY, ICY = range(12)
NICE = 12
WET_ROW = WX
LANES = 128
TRACER_LANE = NICE * NSUB


def even(axis):
    return lax.rem(lax.axis_index(axis), 2) == 0


def spec(shape, index=None):
    zeros = (0,) * len(shape) if index is None else index
    return pl.BlockSpec(shape, lambda *_: zeros)


def vmem():
    return pl.BlockSpec(memory_space=pltpu.VMEM)


def pack_kernel(warm, salt, ocean, wind, ice, cover, volume, wet, icy, planes, inner, outer):
    levels, rows, _ = warm.shape
    for k in range(5):
        planes[U + k] = ice[k]
    planes[UO] = ocean[0]
    planes[VO] = ocean[1]
    planes[AREA] = cover[0] + cover[1] + cover[2] + cover[3] + cover[4]
    planes[THICK] = volume[0] + volume[1] + volume[2] + volume[3] + volume[4]
    planes[WX] = wind[0]
    planes[WY] = wind[1]
    planes[ICY] = icy[...].astype(jnp.float32)

    def eastward(out):
        for p in range(NICE):
            out[NSUB * p : NSUB * (p + 1), :] = planes[p, rows - NSUB :, :]
        at = NSUB * WET_ROW
        out[at : at + 1, :] = wet[rows - 1 :, :].astype(jnp.float32)
        out[NICE * NSUB : NICE * NSUB + levels, :] = warm[:, rows - 1, :]
        out[NICE * NSUB + levels :, :] = salt[:, rows - 1, :]

    def westward(out):
        for p in range(NICE):
            out[NSUB * p : NSUB * (p + 1), :] = planes[p, :NSUB, :]
        at = NSUB * WET_ROW + NSUB - 1
        out[at : at + 1, :] = wet[:1, :].astype(jnp.float32)
        out[NICE * NSUB : NICE * NSUB + levels, :] = warm[:, 0, :]
        out[NICE * NSUB + levels :, :] = salt[:, 0, :]

    @pl.when(even("grp"))
    def _():
        eastward(inner)
        westward(outer)

    @pl.when(jnp.logical_not(even("grp")))
    def _():
        westward(inner)
        eastward(outer)


def columns_kernel(warm, salt, wet, planes, inner, outer, edge, first, second):
    levels, rows, cols = warm.shape

    def place(east, west):
        for p in range(NICE):
            edge[p, :NSUB, :] = east[NSUB * p : NSUB * (p + 1), :]
            edge[p, NSUB:, :] = west[NSUB * p : NSUB * (p + 1), :]

    @pl.when(even("grp"))
    def _():
        place(inner, outer)

    @pl.when(jnp.logical_not(even("grp")))
    def _():
        place(outer, inner)

    def gathered(source, count):
        lane = lax.broadcasted_iota(jnp.int32, (count, LANES), 1)
        low = jnp.zeros((count, LANES), jnp.float32)
        high = low
        for p in range(NICE):
            here = (lane >= NSUB * p) & (lane < NSUB * (p + 1))
            low = jnp.where(here, pltpu.roll(source[p, :, :LANES], NSUB * p, 1), low)
            high = jnp.where(
                here, pltpu.roll(source[p, :, cols - LANES :], NSUB * (p + 1), 1), high
            )
        return lane, low, high

    lane, low, high = gathered(planes, rows)
    for p in range(2 * levels + 1):
        if p < levels:
            left, right = warm[p, :, :LANES], warm[p, :, cols - LANES :]
        elif p < 2 * levels:
            left, right = salt[p - levels, :, :LANES], salt[p - levels, :, cols - LANES :]
        else:
            left = wet[:, :LANES].astype(jnp.float32)
            right = wet[:, cols - LANES :].astype(jnp.float32)
        at = TRACER_LANE + p
        low = jnp.where(lane == at, pltpu.roll(left, at, 1), low)
        high = jnp.where(lane == at, pltpu.roll(right, at + 1, 1), high)
    _, low_edge, high_edge = gathered(edge, 2 * NSUB)
    north_first = even("gy")
    first[:rows, :] = jnp.where(north_first, high, low)
    first[rows:, :] = jnp.where(north_first, high_edge, low_edge)
    second[:rows, :] = jnp.where(north_first, low, high)
    second[rows:, :] = jnp.where(north_first, low_edge, high_edge)


def sides(first, second):
    north_first = even("gy")
    one, two = first[...], second[...]
    return jnp.where(north_first, two, one), jnp.where(north_first, one, two)


def columns_of(low, high, p):
    lane = lax.broadcasted_iota(jnp.int32, low.shape, 1)
    above = high if p == 0 else pltpu.roll(high, LANES - NSUB * p, 1)
    below = pltpu.roll(low, LANES - NSUB * (p + 1), 1)
    return jnp.where(lane < NSUB, above, jnp.where(lane >= LANES - NSUB, below, 0.0))


def ice_kernel(planes, edge, first, second, wet, home, velocity, picked):
    rows, cols = wet.shape
    pieces = cols // LANES
    tall = rows + 2 * NSUB
    broad = cols + LANES
    low, high = sides(first, second)
    wide = [
        jnp.concatenate(
            [jnp.concatenate([planes[p], edge[p]], axis=0), columns_of(low, high, p)], axis=1
        )
        for p in range(NICE)
    ]
    east = lambda f: pltpu.roll(f, tall - 1, 0)
    west = lambda f: pltpu.roll(f, 1, 0)
    north = lambda f: pltpu.roll(f, broad - 1, 1)
    south = lambda f: pltpu.roll(f, 1, 1)
    area, thick, mask = wide[AREA], wide[THICK], wide[ICY]
    strength = (thick * jnp.exp(-STRENGTH_COEF * (1.0 - area))) * RELAX_RATE
    mass = thick + MIN_MASS
    keep = mask * (1.0 / (1.0 + RELAX_RATE))
    ocean_u, ocean_v = wide[UO], wide[VO]
    u, v, s1, s2, s12 = (wide[k] for k in range(5))
    for _ in range(NSUB):
        du, dv = east(u) - u, north(v) - v
        div, ten = du + dv, du - dv
        shr = (north(u) - u) + (east(v) - v)
        visc = strength * lax.rsqrt(
            div * div + (ten * ten + shr * shr) * (1.0 / ECCENTRIC) + DELTA_FLOOR
        )
        quarter = visc * (1.0 / ECCENTRIC)
        s1 = keep * (s1 + (visc * div - strength))
        s2 = keep * (s2 + quarter * ten)
        s12 = keep * (s12 + quarter * shr)
        total, gap = s1 + s2, s1 - s2
        force_u = 0.5 * (total - west(total)) + (s12 - south(s12))
        force_v = 0.5 * (gap - south(gap)) + (s12 - west(s12))
        coef = area * jnp.sqrt((ocean_u - u) ** 2 + (ocean_v - v) ** 2 + SPEED_FLOOR)
        scale = mask / (mass + coef)
        turn = CORIOLIS * mass
        u, v = (
            scale * (mass * u + force_u + wide[WX] + coef * ocean_u + turn * v),
            scale * (mass * v + force_v + wide[WY] + coef * ocean_v - turn * u),
        )
    own = lambda f: f[:rows, :cols]
    u, v, ocean_u, ocean_v = own(u), own(v), own(ocean_u), own(ocean_v)
    coef = own(area) * jnp.sqrt((ocean_u - u) ** 2 + (ocean_v - v) ** 2 + SPEED_FLOOR)
    drag = (STRESS_SCALE * own(mask)) * coef
    sea = wet[...].astype(jnp.float32)
    velocity[0] = sea * (ocean_u + drag * (u - ocean_u))
    velocity[1] = sea * (ocean_v + drag * (v - ocean_v))
    for k, f in enumerate((u, v, own(s1), own(s2), own(s12))):
        blocks = [f[:, LANES * b : LANES * (b + 1)] for b in range(pieces)]
        for owner in range(pieces):
            value = jnp.zeros_like(blocks[0])
            for b in range(pieces):
                value = jnp.where(home[0, b] == owner, blocks[b], value)
            picked[owner, k] = value


def tracer_kernel(
    warm, salt, wet, icy, cover, volume, first, second, inner, outer,
    warm_out, salt_out, coef, cut_low, cut_high, gain, rise,
):
    step = pl.program_id(0)
    levels, rows, cols = warm.shape
    count = warm_out.shape[0]
    low, high = sides(first, second)
    low, high = low[:rows], high[:rows]
    top = NICE * NSUB

    @pl.when(step == 0)
    def _():
        lane = lax.broadcasted_iota(jnp.int32, (rows, cols), 1)
        row = lax.broadcasted_iota(jnp.int32, (rows, cols), 0)
        short = lax.broadcasted_iota(jnp.int32, (rows, LANES), 1)
        sea = wet[...].astype(jnp.float32)
        mine = DIFFUSIVITY * sea
        east = jnp.where(row < rows - 1, mine * pltpu.roll(sea, rows - 1, 0), 0.0)
        west = jnp.where(row > 0, mine * pltpu.roll(sea, 1, 0), 0.0)
        north = jnp.where(lane < cols - 1, mine * pltpu.roll(sea, cols - 1, 1), 0.0)
        south = jnp.where(lane > 0, mine * pltpu.roll(sea, 1, 1), 0.0)
        at = TRACER_LANE + 2 * levels
        edge_low = jnp.where(short == 0, mine[:, :LANES] * pltpu.roll(low, LANES - at, 1), 0.0)
        edge_high = jnp.where(
            short == LANES - 1,
            mine[:, cols - LANES :] * pltpu.roll(high, LANES - 1 - at, 1),
            0.0,
        )
        coef[1], coef[2], coef[3], coef[4] = east, west, north, south
        coef[0] = 1.0 - (east + west + north + south)
        coef[0, :, :LANES] -= edge_low
        coef[0, :, cols - LANES :] -= edge_high
        cut_low[...], cut_high[...] = edge_low, edge_high
        last, head = NSUB * WET_ROW + NSUB - 1, NSUB * WET_ROW

        def fluxes(from_east, from_west):
            east_gain = mine[rows - 1 :, :] * from_east[last : last + 1, :]
            west_gain = mine[:1, :] * from_west[head : head + 1, :]
            coef[0, rows - 1 :, :] -= east_gain
            coef[0, :1, :] -= west_gain
            rise[...] = east_gain * from_east[top:, :]
            gain[...] = west_gain * from_west[top:, :]

        @pl.when(even("grp"))
        def _():
            fluxes(inner, outer)

        @pl.when(jnp.logical_not(even("grp")))
        def _():
            fluxes(outer, inner)

    for part, (field, out) in enumerate(((warm, warm_out), (salt, salt_out))):
        for k in range(count):
            level = step * count + k
            f = field[level]
            out[k] = (
                coef[0] * f
                + coef[1] * pltpu.roll(f, rows - 1, 0)
                + coef[2] * pltpu.roll(f, 1, 0)
                + coef[3] * pltpu.roll(f, cols - 1, 1)
                + coef[4] * pltpu.roll(f, 1, 1)
            )
            plane = part * levels + level
            at = TRACER_LANE + plane
            out[k, :, :LANES] += cut_low[...] * pltpu.roll(low, LANES - at, 1)
            out[k, :, cols - LANES :] += cut_high[...] * pltpu.roll(high, LANES - 1 - at, 1)
            out[k, rows - 1 :, :] += rise[pl.ds(plane, 1), :]
            out[k, :1, :] += gain[pl.ds(plane, 1), :]

    @pl.when(step == 0)
    def _():
        heat = jnp.zeros((rows, cols), jnp.float32)
        for k in range(cover.shape[0]):
            heat += HEAT_COEF * cover[k] * cover[k] / (volume[k] + THIN_LIMIT * cover[k])
        heat *= icy[...].astype(jnp.float32) * (warm[0] - FREEZING)
        warm_out[0] -= WARMTH_FACTOR * wet[...].astype(jnp.float32) * heat


def place_kernel(pieces, out):
    for y in range(pieces.shape[0]):
        out[:, :, LANES * y : LANES * (y + 1)] = pieces[y]


def float_like(*shape):
    return jax.ShapeDtypeStruct(shape, jnp.float32)


def near(*shape):
    return pltpu.VMEM(shape, jnp.float32)


def held(*arrays):
    return tuple(pltpu.with_memory_space_constraint(a, pltpu.VMEM) for a in arrays)


def per_device(
    warm, salt, ocean, wind, ice, cover, volume, wet, icy, home
):
    levels, rows, cols = warm.shape
    grp, gy = lax.axis_size("grp"), lax.axis_size("gy")
    assert grp % 2 == 0 and gy % 2 == 0 and cols == gy * LANES
    swap = lambda pairs: [p for i, j in pairs for p in ((i, j), (j, i))]
    inner_pairs = swap([(i, i + 1) for i in range(0, grp, 2)])
    outer_pairs = swap([(i, (i + 1) % grp) for i in range(1, grp, 2)])
    first_pairs = swap([(i, i + 1) for i in range(0, gy, 2)])
    second_pairs = swap([(i, i + 1) for i in range(1, gy - 1, 2)])
    tall = rows + 2 * NSUB
    tile = near(tall, LANES)
    message = near(NICE * NSUB + 2 * levels, cols)


    planes, inner, outer = pl.pallas_call(
        pack_kernel,
        out_shape=[near(NICE, rows, cols), message, message],
        in_specs=[vmem()] * 9,
        out_specs=[vmem()] * 3,
        name="pack",
    )(warm, salt, ocean, wind, ice, cover, volume, wet, icy)
    outer = lax.ppermute(outer, "grp", outer_pairs)
    inner = lax.ppermute(inner, "grp", inner_pairs)

    edge, first, second = pl.pallas_call(
        columns_kernel,
        out_shape=[near(NICE, 2 * NSUB, cols), tile, tile],
        in_specs=[vmem()] * 6,
        out_specs=[vmem()] * 3,
        name="columns",
    )(warm, salt, wet, *held(planes, inner, outer))
    first = lax.ppermute(first, "gy", first_pairs)
    second = lax.ppermute(second, "gy", second_pairs)

    velocity, picked = pl.pallas_call(
        ice_kernel,
        out_shape=[float_like(2, rows, cols), float_like(gy, 5, rows, LANES)],
        in_specs=[vmem()] * 5 + [pl.BlockSpec(memory_space=pltpu.SMEM)],
        out_specs=[vmem()] * 2,
        name="ice",
    )(*held(planes, edge, first, second), wet, home)
    owned = lax.all_to_all(picked, "gy", split_axis=0, concat_axis=0, tiled=True)

    steps = 4
    block = pl.BlockSpec((levels // steps, rows, cols), lambda i: (i, 0, 0))
    warm_out, salt_out = pl.pallas_call(
        tracer_kernel,
        grid=(steps,),
        in_specs=[
            vmem(), vmem(), spec(wet.shape), spec(icy.shape), spec(cover.shape), spec(volume.shape),
            vmem(), vmem(), vmem(), vmem(),
        ],
        out_specs=[block, block],
        out_shape=[float_like(*warm.shape), float_like(*salt.shape)],
        scratch_shapes=[
            pltpu.VMEM((5, rows, cols), jnp.float32),
            pltpu.VMEM((rows, LANES), jnp.float32),
            pltpu.VMEM((rows, LANES), jnp.float32),
            pltpu.VMEM((2 * levels, cols), jnp.float32),
            pltpu.VMEM((2 * levels, cols), jnp.float32),
        ],
        name="tracers",
    )(warm, salt, wet, icy, cover, volume, *held(first, second, inner, outer))

    patch = pl.pallas_call(
        place_kernel,
        out_shape=float_like(5, rows, cols),
        in_specs=[vmem()],
        out_specs=vmem(),
        name="place",
    )(*held(owned))
    return warm_out, salt_out, velocity, patch


def solution(mesh):
    field = P(None, "grp", "gy")
    flat = P("grp", "gy")

    return jax.shard_map(
        per_device,
        mesh=mesh,
        in_specs=(field,) * 7 + (flat,) * 3,
        out_specs=(field,) * 4,
        check_vma=False,
    )
```

time: 80.6 us -> 53.2 us (0.66)
  other arithmetic: 21.4 us -> 0 us
  Pallas kernels: 0 us -> 10.9 us
  local copies, waits for them, and re-layouts: 10.6 us -> 0 us
  starting transfers between devices: 35.8 us -> 32.6 us
  waiting for transfers between devices: 10.5 us -> 8.52 us
    pallas_call x0 -> x5, Pallas kernels: none -> 10.9 us  [the longest x1 4.22 us: per_device(): pl.pallas_call(tracer_kernel, grid=(steps,), in_specs=[vmem(), vmem(), sp...]
    add x1 -> x0, other arithmetic: 8.08 us -> none  [diffuse_tile(): return centre + DIFFUSIVITY * wet_wide[1:-1, 1:-1] * inflow]
    slice x52 -> x0, local copies, waits for them, and re-layouts: 3.64 us -> none  [the longest x2 1.19 us: extended(): lax.slice_in_dim(cells, cells.shape[dim] - width, cells.shape[dim], axis=...]
    div x14 -> x0, other arithmetic: 3.54 us -> none  [the longest x3 0.99 us: evp_subcycles(): glacial_indicator * (ice_mass * vel_v + force_v + wind_v + water_coef * c...]
    select_n x1 -> x0, other arithmetic: 3.42 us -> none  [close_rims(): return jnp.where(low_rim | high_rim, 0.0, padded)]
    all_to_all x1, starting transfers between devices: 7.45 us -> 4.08 us  [per_device(): lax.all_to_all(picked, 'gy', split_axis=0, concat_axis=0, tiled=True)]
    ppermute x4, waiting for transfers between devices: 10.5 us -> 7.32 us  [the longest x1 4.99 us: per_device(): outer = lax.ppermute(outer, 'grp', outer_pairs)]
    unnamed x43 -> x0, local copies, waits for them, and re-layouts: 2.67 us -> none
  transfers between devices with their start and end apart: 5 -> 5, of which waited for: 2 -> 4; matrix products, arithmetic and copies ran while one was open for 15% -> 0% of each run, Pallas kernels for 0% -> 8%
where the time goes in v1:
time: 53.2 us; the launch traced here: 52.7 us
  starting transfers between devices  32.6 us (61%)
  Pallas kernels  10.9 us (20%)
  waiting for transfers between devices  8.52 us (16%)
  between operations  0.69 us (1%)
    ppermute x1, starting transfers between devices, per_device(): outer = lax.ppermute(outer, 'grp', outer_pairs)  21.2 us
    ppermute x1, waiting for transfers between devices, per_device(): outer = lax.ppermute(outer, 'grp', outer_pairs)  4.99 us
    pallas_call x1, Pallas kernels, per_device(): pl.pallas_call(tracer_kernel, grid=(steps,), in_specs=[vmem(), vmem(), sp...  4.22 us
    all_to_all x1, starting transfers between devices, per_device(): lax.all_to_all(picked, 'gy', split_axis=0, concat_axis=0, tiled=True)  4.08 us
    ppermute x1, starting transfers between devices, per_device(): second = lax.ppermute(second, 'gy', second_pairs)  3.26 us
    pallas_call x1, Pallas kernels, per_device(): pl.pallas_call(ice_kernel, out_shape=[float_like(2, rows, cols), float_li...  2.52 us
    ppermute x1, waiting for transfers between devices, per_device(): second = lax.ppermute(second, 'gy', second_pairs)  2.14 us
    ppermute x1, starting transfers between devices, per_device(): first = lax.ppermute(first, 'gy', first_pairs)  2.13 us
  transfers between devices with their start and end apart: 5, of which 4 were waited for; matrix products, arithmetic and copies ran while one was open for 0% of the time, Pallas kernels for 8%

profile of v1, /device:TPU:8, one launch (start us, length us, event | category | flops | bytes accessed | tf_op | source)
XLA Modules:
  0.0 52.7 jit_solution(13397161756517292604)
XLA Ops:
  0.6 1.7 %pack.1 = (f32[12,16,512]{2,1,0:T(8,128)S(1)}, f32[96,512]{1,0:T(8,128)S(1)}, f32[96,512]{1,0:T(8,128)S(1)}) custom-call(f32[24,16,512]{2,1,0:T(8,128)} %warm.5, f32[24,16,512]{2,1,0:T(8,128)} %salt.5, f32[2,16,512]{2,1,0:T(8,128)} %ocean.1, f32[2,16,512]{2,1,0:T(8,128)} %wind.1, f32[5,16,512]{2,1,0:T(8,128)} %ice.2, f32[5,16,512]{2,1,0:T(8,128)} %cover.3, ...), custom_call_target="tpu_custom_call" | custom-call | tf_op jit(solution)/shard_map/pack/pallas_call | solution.py:315
  2.3 1.9 %collective-permute-start = (f32[96,512]{1,0:T(8,128)S(1)}, f32[96,512]{1,0:T(8,128)S(1)}, u32[]{:S(2)}, u32[]{:S(2)}) collective-permute-start(f32[96,512]{1,0:T(8,128)S(1)} %get-tuple-element.15), channel_id=1, source_target_pairs={{0,4},{4,0},{8,12},{12,8},{16,20},{20,16},{24,28},{28,24},{32,36},... | collective-permute-start | bytes 589832 | tf_op jit(solution)/shard_map/ppermute | solution.py:323
  4.2 21.2 %collective-permute-start.1 = (f32[96,512]{1,0:T(8,128)S(1)}, f32[96,512]{1,0:T(8,128)S(1)}, u32[]{:S(2)}, u32[]{:S(2)}) collective-permute-start(f32[96,512]{1,0:T(8,128)S(1)} %get-tuple-element.16), channel_id=1, source_target_pairs={{4,8},{8,4},{12,16},{16,12},{20,24},{24,20},{28,32},{32,28},{36,40... | collective-permute-start | bytes 589832 | tf_op jit(solution)/shard_map/ppermute | solution.py:322
  25.5 0.0 collective-permute-done.inner
  25.5 5.0 %collective-permute-done.1.outer = f32[96,512]{1,0:T(8,128)S(1)} collective-permute-done((f32[96,512]{1,0:T(8,128)S(1)}, f32[96,512]{1,0:T(8,128)S(1)}, u32[]{:S(2)}, u32[]{:S(2)}) %collective-permute-start.1) | collective-permute-done | bytes 196640 | tf_op jit(solution)/shard_map/ppermute | solution.py:322
  30.5 1.8 %columns.1 = (f32[12,8,512]{2,1,0:T(8,128)S(1)}, f32[24,128]{1,0:T(8,128)S(1)}, f32[24,128]{1,0:T(8,128)S(1)}) custom-call(f32[24,16,512]{2,1,0:T(8,128)} %warm.5, f32[24,16,512]{2,1,0:T(8,128)} %salt.5, s32[16,512]{1,0:T(8,128)} %wet.7, f32[12,16,512]{2,1,0:T(8,128)S(1)} %get-tuple-element.14.planes, f32[96,512]{1,0:T(8,128)S(1)} %collective-permute-done.inner, ...), custom_call_target="tpu_custom_call" | custom-call | tf_op jit(solution)/shard_map/columns/pallas_call | solution.py:325
  32.3 2.1 %collective-permute-start.2 = (f32[24,128]{1,0:T(8,128)S(1)}, f32[24,128]{1,0:T(8,128)S(1)}, u32[]{:S(2)}, u32[]{:S(2)}) collective-permute-start(f32[24,128]{1,0:T(8,128)S(1)} %get-tuple-element.17), channel_id=1, source_target_pairs={{0,1},{1,0},{2,3},{3,2},{4,5},{5,4},{6,7},{7,6},{8,9},{9,8},{10,11... | collective-permute-start | bytes 36872 | tf_op jit(solution)/shard_map/ppermute | solution.py:332
  34.4 3.3 %collective-permute-start.3 = (f32[24,128]{1,0:T(8,128)S(1)}, f32[24,128]{1,0:T(8,128)S(1)}, u32[]{:S(2)}, u32[]{:S(2)}) collective-permute-start(f32[24,128]{1,0:T(8,128)S(1)} %get-tuple-element.18), channel_id=1, source_target_pairs={{1,2},{2,1},{5,6},{6,5},{9,10},{10,9},{13,14},{14,13},{17,18},{18,... | collective-permute-start | bytes 36872 | tf_op jit(solution)/shard_map/ppermute | solution.py:333
  37.7 0.2 collective-permute-done.2.first
  37.9 2.1 %collective-permute-done.3.second = f32[24,128]{1,0:T(8,128)S(1)} collective-permute-done((f32[24,128]{1,0:T(8,128)S(1)}, f32[24,128]{1,0:T(8,128)S(1)}, u32[]{:S(2)}, u32[]{:S(2)}) %collective-permute-start.3) | collective-permute-done | bytes 12320 | tf_op jit(solution)/shard_map/ppermute | solution.py:333
  40.0 2.5 %ice.3 = (f32[2,16,512]{2,1,0:T(8,128)}, f32[4,5,16,128]{3,2,1,0:T(8,128)}) custom-call(f32[12,16,512]{2,1,0:T(8,128)S(1)} %get-tuple-element.14.planes, f32[12,8,512]{2,1,0:T(8,128)S(1)} %get-tuple-element.21.edge, f32[24,128]{1,0:T(8,128)S(1)} %collective-permute-done.2.first, f32[24,128]{1,0:T(8,128)S(1)} %collective-permute-done.3.second, ...), custom_call_target="tpu_custom_call" | custom-call | tf_op jit(solution)/shard_map/ice/pallas_call | solution.py:335
  42.5 4.1 %all-to-all-start = ((f32[4,5,16,128]{3,2,1,0:T(8,128)}), f32[4,5,16,128]{3,2,1,0:T(8,128)S(1)}, u32[]{:S(2)}, u32[]{:S(2)}) async-start(f32[4,5,16,128]{3,2,1,0:T(8,128)} %get-tuple-element.23), calls=%async_computation | async-start | bytes 327680 | tf_op jit(solution)/shard_map/all_to_all | solution.py:342
  46.6 4.2 %tracers.1 = (f32[24,16,512]{2,1,0:T(8,128)}, f32[24,16,512]{2,1,0:T(8,128)}) custom-call(f32[24,16,512]{2,1,0:T(8,128)} %warm.5, f32[24,16,512]{2,1,0:T(8,128)} %salt.5, s32[16,512]{1,0:T(8,128)} %wet.7, s32[16,512]{1,0:T(8,128)} %icy.3, f32[5,16,512]{2,1,0:T(8,128)} %cover.3, f32[5,16,512]{2,1,0:T(8,128)} %volume.3, ...), custom_call_target="tpu_custom_call" | custom-call | tf_op jit(solution)/shard_map/tracers/pallas_call | solution.py:346
  50.8 1.2 %all-to-all-done.pieces = f32[4,5,16,128]{3,2,1,0:T(8,128)S(1)} async-done(((f32[4,5,16,128]{3,2,1,0:T(8,128)}), f32[4,5,16,128]{3,2,1,0:T(8,128)S(1)}, u32[]{:S(2)}, u32[]{:S(2)}) %all-to-all-start) | async-done | bytes 163872 | tf_op jit(solution)/shard_map/all_to_all | solution.py:342
  52.0 0.7 %place.1 = f32[5,16,512]{2,1,0:T(8,128)} custom-call(f32[4,5,16,128]{3,2,1,0:T(8,128)S(1)} %all-to-all-done.pieces), custom_call_target="tpu_custom_call" | custom-call | tf_op jit(solution)/shard_map/place/pallas_call | solution.py:365
Async XLA Ops:
  2.3 23.2 %collective-permute-start = (f32[96,512]{1,0:T(8,128)S(1)}, f32[96,512]{1,0:T(8,128)S(1)}, u32[]{:S(2)}, u32[]{:S(2)}) collective-permute-start(f32[96,512]{1,0:T(8,128)S(1)} %get-tuple-element.15), channel_id=1, source_target_pairs={{0,4},{4,0},{8,12},{12,8},{16,20},{20,16},{24,28},{28,24},{32,36},... | collective-permute-start | bytes 589832 | tf_op jit(solution)/shard_map/ppermute | solution.py:323
  4.2 26.3 %collective-permute-start.1 = (f32[96,512]{1,0:T(8,128)S(1)}, f32[96,512]{1,0:T(8,128)S(1)}, u32[]{:S(2)}, u32[]{:S(2)}) collective-permute-start(f32[96,512]{1,0:T(8,128)S(1)} %get-tuple-element.16), channel_id=1, source_target_pairs={{4,8},{8,4},{12,16},{16,12},{20,24},{24,20},{28,32},{32,28},{36,40... | collective-permute-start | bytes 589832 | tf_op jit(solution)/shard_map/ppermute | solution.py:322
  32.3 5.6 %collective-permute-start.2 = (f32[24,128]{1,0:T(8,128)S(1)}, f32[24,128]{1,0:T(8,128)S(1)}, u32[]{:S(2)}, u32[]{:S(2)}) collective-permute-start(f32[24,128]{1,0:T(8,128)S(1)} %get-tuple-element.17), channel_id=1, source_target_pairs={{0,1},{1,0},{2,3},{3,2},{4,5},{5,4},{6,7},{7,6},{8,9},{9,8},{10,11... | collective-permute-start | bytes 36872 | tf_op jit(solution)/shard_map/ppermute | solution.py:332
  34.4 5.6 %collective-permute-start.3 = (f32[24,128]{1,0:T(8,128)S(1)}, f32[24,128]{1,0:T(8,128)S(1)}, u32[]{:S(2)}, u32[]{:S(2)}) collective-permute-start(f32[24,128]{1,0:T(8,128)S(1)} %get-tuple-element.18), channel_id=1, source_target_pairs={{1,2},{2,1},{5,6},{6,5},{9,10},{10,9},{13,14},{14,13},{17,18},{18,... | collective-permute-start | bytes 36872 | tf_op jit(solution)/shard_map/ppermute | solution.py:333
  42.5 9.5 %all-to-all-start = ((f32[4,5,16,128]{3,2,1,0:T(8,128)}), f32[4,5,16,128]{3,2,1,0:T(8,128)S(1)}, u32[]{:S(2)}, u32[]{:S(2)}) async-start(f32[4,5,16,128]{3,2,1,0:T(8,128)} %get-tuple-element.23), calls=%async_computation | async-start | bytes 327680 | tf_op jit(solution)/shard_map/all_to_all | solution.py:342

commit v2 on v1

--- a/solution.py
+++ b/solution.py
@@ -41,47 +41,113 @@
     return pl.BlockSpec(memory_space=pltpu.VMEM)
 
 
-def pack_kernel(warm, salt, ocean, wind, ice, cover, volume, wet, icy, planes, inner, outer):
+def outer_kernel(*refs):
+    fields, warm, salt, out = refs[:7], refs[7], refs[8], refs[9]
+    tiles, sems, row_sems = refs[10:17], refs[17], refs[18]
     levels, rows, _ = warm.shape
+    half = rows // 2
+    top = NICE * NSUB
+
+    def message(start, row, wet_slot, edge_row):
+        copies = [
+            pltpu.make_async_copy(f.at[..., start : start + half, :], tile, sems.at[k])
+            for k, (f, tile) in enumerate(zip(fields, tiles))
+        ]
+        lines = [
+            pltpu.make_async_copy(
+                f.at[:, start + edge_row, :], out.at[top + k * levels : top + (k + 1) * levels, :], row_sems.at[k]
+            )
+            for k, f in enumerate((warm, salt))
+        ]
+        for copy in copies + lines:
+            copy.start()
+        for copy in copies:
+            copy.wait()
+        ocean, wind, ice, cover, volume, wet, icy = tiles
+        cut = slice(row, row + NSUB)
+        planes = [ice[k, cut, :] for k in range(5)] + [ocean[0, cut, :], ocean[1, cut, :]]
+        planes += [sum(f[k, cut, :] for k in range(f.shape[0])) for f in (cover, volume)]
+        planes += [wind[0, cut, :], wind[1, cut, :], icy[cut, :].astype(jnp.float32)]
+        for p in range(NICE):
+            out[NSUB * p : NSUB * (p + 1), :] = planes[p]
+        at = NSUB * WET_ROW + wet_slot
+        out[at : at + 1, :] = wet[edge_row : edge_row + 1, :].astype(jnp.float32)
+        for copy in lines:
+            copy.wait()
+
+    @pl.when(even("grp"))
+    def _():
+        message(0, 0, NSUB - 1, 0)
+
+    @pl.when(jnp.logical_not(even("grp")))
+    def _():
+        message(half, half - NSUB, 0, half - 1)
+
+
+def gathered(source, count):
+    cols = source.shape[2]
+    lane = lax.broadcasted_iota(jnp.int32, (count, LANES), 1)
+    low = jnp.zeros((count, LANES), jnp.float32)
+    high = low
+    for p in range(NICE):
+        here = (lane >= NSUB * p) & (lane < NSUB * (p + 1))
+        low = jnp.where(here, pltpu.roll(source[p, :, :LANES], NSUB * p, 1), low)
+        high = jnp.where(here, pltpu.roll(source[p, :, cols - LANES :], NSUB * (p + 1), 1), high)
+    return lane, low, high
+
+
+def inner_kernel(
+    warm, salt, ocean, wind, ice, cover, volume, wet, icy, home,
+    planes, inner, low_out, high_out, sea, chosen,
+):
+    levels, rows, cols = warm.shape
     for k in range(5):
         planes[U + k] = ice[k]
     planes[UO] = ocean[0]
     planes[VO] = ocean[1]
-    planes[AREA] = cover[0] + cover[1] + cover[2] + cover[3] + cover[4]
-    planes[THICK] = volume[0] + volume[1] + volume[2] + volume[3] + volume[4]
+    planes[AREA] = sum(cover[k] for k in range(cover.shape[0]))
+    planes[THICK] = sum(volume[k] for k in range(volume.shape[0]))
     planes[WX] = wind[0]
     planes[WY] = wind[1]
     planes[ICY] = icy[...].astype(jnp.float32)
-
-    def eastward(out):
+    sea[...] = wet[...].astype(jnp.float32)
+    blocks = home.shape[1]
+    for owner in range(blocks):
+        for b in range(blocks):
+            flag = jnp.where(home[0, b] == owner, 1.0, 0.0)
+            chosen[owner * blocks + b] = jnp.full(chosen.shape[1:], flag, jnp.float32)
+
+    def message(row, wet_slot, edge_row):
         for p in range(NICE):
-            out[NSUB * p : NSUB * (p + 1), :] = planes[p, rows - NSUB :, :]
-        at = NSUB * WET_ROW
-        out[at : at + 1, :] = wet[rows - 1 :, :].astype(jnp.float32)
-        out[NICE * NSUB : NICE * NSUB + levels, :] = warm[:, rows - 1, :]
-        out[NICE * NSUB + levels :, :] = salt[:, rows - 1, :]
-
-    def westward(out):
-        for p in range(NICE):
-            out[NSUB * p : NSUB * (p + 1), :] = planes[p, :NSUB, :]
-        at = NSUB * WET_ROW + NSUB - 1
-        out[at : at + 1, :] = wet[:1, :].astype(jnp.float32)
-        out[NICE * NSUB : NICE * NSUB + levels, :] = warm[:, 0, :]
-        out[NICE * NSUB + levels :, :] = salt[:, 0, :]
+            inner[NSUB * p : NSUB * (p + 1), :] = planes[p, row : row + NSUB, :]
+        at = NSUB * WET_ROW + wet_slot
+        inner[at : at + 1, :] = sea[edge_row : edge_row + 1, :]
+        inner[NICE * NSUB : NICE * NSUB + levels, :] = warm[:, edge_row, :]
+        inner[NICE * NSUB + levels :, :] = salt[:, edge_row, :]
 
     @pl.when(even("grp"))
     def _():
-        eastward(inner)
-        westward(outer)
+        message(rows - NSUB, 0, rows - 1)
 
     @pl.when(jnp.logical_not(even("grp")))
     def _():
-        westward(inner)
-        eastward(outer)
-
-
-def columns_kernel(warm, salt, wet, planes, inner, outer, edge, first, second):
-    levels, rows, cols = warm.shape
+        message(0, NSUB - 1, 0)
+
+    lane, low, high = gathered(planes, rows)
+    for p in range(2 * levels + 1):
+        if p < 2 * levels:
+            field = warm[p] if p < levels else salt[p - levels]
+        else:
+            field = sea[...]
+        at = TRACER_LANE + p
+        low = jnp.where(lane == at, pltpu.roll(field[:, :LANES], at, 1), low)
+        high = jnp.where(lane == at, pltpu.roll(field[:, cols - LANES :], at + 1, 1), high)
+    low_out[...] = low
+    high_out[...] = high
+
+
+def edge_kernel(inner, outer, low, high, edge, first, second):
+    rows = low.shape[0]
 
     def place(east, west):
         for p in range(NICE):
@@ -96,35 +162,11 @@
     def _():
         place(outer, inner)
 
-    def gathered(source, count):
-        lane = lax.broadcasted_iota(jnp.int32, (count, LANES), 1)
-        low = jnp.zeros((count, LANES), jnp.float32)
-        high = low
-        for p in range(NICE):
-            here = (lane >= NSUB * p) & (lane < NSUB * (p + 1))
-            low = jnp.where(here, pltpu.roll(source[p, :, :LANES], NSUB * p, 1), low)
-            high = jnp.where(
-                here, pltpu.roll(source[p, :, cols - LANES :], NSUB * (p + 1), 1), high
-            )
-        return lane, low, high
-
-    lane, low, high = gathered(planes, rows)
-    for p in range(2 * levels + 1):
-        if p < levels:
-            left, right = warm[p, :, :LANES], warm[p, :, cols - LANES :]
-        elif p < 2 * levels:
-            left, right = salt[p - levels, :, :LANES], salt[p - levels, :, cols - LANES :]
-        else:
-            left = wet[:, :LANES].astype(jnp.float32)
-            right = wet[:, cols - LANES :].astype(jnp.float32)
-        at = TRACER_LANE + p
-        low = jnp.where(lane == at, pltpu.roll(left, at, 1), low)
-        high = jnp.where(lane == at, pltpu.roll(right, at + 1, 1), high)
     _, low_edge, high_edge = gathered(edge, 2 * NSUB)
     north_first = even("gy")
-    first[:rows, :] = jnp.where(north_first, high, low)
+    first[:rows, :] = jnp.where(north_first, high[...], low[...])
     first[rows:, :] = jnp.where(north_first, high_edge, low_edge)
-    second[:rows, :] = jnp.where(north_first, low, high)
+    second[:rows, :] = jnp.where(north_first, low[...], high[...])
     second[rows:, :] = jnp.where(north_first, low_edge, high_edge)
 
 
@@ -141,8 +183,12 @@
     return jnp.where(lane < NSUB, above, jnp.where(lane >= LANES - NSUB, below, 0.0))
 
 
-def ice_kernel(planes, edge, first, second, wet, home, velocity, picked):
-    rows, cols = wet.shape
+def root(square):
+    return square * lax.rsqrt(square)
+
+
+def ice_kernel(planes, edge, first, second, sea, chosen, velocity, picked):
+    rows, cols = sea.shape
     pieces = cols // LANES
     tall = rows + 2 * NSUB
     broad = cols + LANES
@@ -177,7 +223,7 @@
         total, gap = s1 + s2, s1 - s2
         force_u = 0.5 * (total - west(total)) + (s12 - south(s12))
         force_v = 0.5 * (gap - south(gap)) + (s12 - west(s12))
-        coef = area * jnp.sqrt((ocean_u - u) ** 2 + (ocean_v - v) ** 2 + SPEED_FLOOR)
+        coef = area * root((ocean_u - u) ** 2 + (ocean_v - v) ** 2 + SPEED_FLOOR)
         scale = mask / (mass + coef)
         turn = CORIOLIS * mass
         u, v = (
@@ -186,23 +232,23 @@
         )
     own = lambda f: f[:rows, :cols]
     u, v, ocean_u, ocean_v = own(u), own(v), own(ocean_u), own(ocean_v)
-    coef = own(area) * jnp.sqrt((ocean_u - u) ** 2 + (ocean_v - v) ** 2 + SPEED_FLOOR)
+    coef = own(area) * root((ocean_u - u) ** 2 + (ocean_v - v) ** 2 + SPEED_FLOOR)
     drag = (STRESS_SCALE * own(mask)) * coef
-    sea = wet[...].astype(jnp.float32)
-    velocity[0] = sea * (ocean_u + drag * (u - ocean_u))
-    velocity[1] = sea * (ocean_v + drag * (v - ocean_v))
+    velocity[0] = sea[...] * (ocean_u + drag * (u - ocean_u))
+    velocity[1] = sea[...] * (ocean_v + drag * (v - ocean_v))
+    here = [jnp.concatenate([chosen[k]] * (rows // 8), axis=0) > 0.5 for k in range(pieces * pieces)]
     for k, f in enumerate((u, v, own(s1), own(s2), own(s12))):
         blocks = [f[:, LANES * b : LANES * (b + 1)] for b in range(pieces)]
         for owner in range(pieces):
             value = jnp.zeros_like(blocks[0])
             for b in range(pieces):
-                value = jnp.where(home[0, b] == owner, blocks[b], value)
+                value = jnp.where(here[owner * pieces + b], blocks[b], value)
             picked[owner, k] = value
 
 
 def tracer_kernel(
-    warm, salt, wet, icy, cover, volume, first, second, inner, outer,
-    warm_out, salt_out, coef, cut_low, cut_high, gain, rise,
+    warm, salt, sea_in, icy, cover, volume, first, second, inner, outer, flow,
+    warm_out, salt_out, flow_out, coef, cut_low, cut_high, gain, rise,
 ):
     step = pl.program_id(0)
     levels, rows, cols = warm.shape
@@ -216,7 +262,8 @@
         lane = lax.broadcasted_iota(jnp.int32, (rows, cols), 1)
         row = lax.broadcasted_iota(jnp.int32, (rows, cols), 0)
         short = lax.broadcasted_iota(jnp.int32, (rows, LANES), 1)
-        sea = wet[...].astype(jnp.float32)
+        flow_out[...] = flow[...]
+        sea = sea_in[...]
         mine = DIFFUSIVITY * sea
         east = jnp.where(row < rows - 1, mine * pltpu.roll(sea, rows - 1, 0), 0.0)
         west = jnp.where(row > 0, mine * pltpu.roll(sea, 1, 0), 0.0)
@@ -276,12 +323,18 @@
         for k in range(cover.shape[0]):
             heat += HEAT_COEF * cover[k] * cover[k] / (volume[k] + THIN_LIMIT * cover[k])
         heat *= icy[...].astype(jnp.float32) * (warm[0] - FREEZING)
-        warm_out[0] -= WARMTH_FACTOR * wet[...].astype(jnp.float32) * heat
-
-
-def place_kernel(pieces, out):
-    for y in range(pieces.shape[0]):
-        out[:, :, LANES * y : LANES * (y + 1)] = pieces[y]
+        warm_out[0] -= WARMTH_FACTOR * sea_in[...] * heat
+
+
+def place_kernel(pieces, out, sems):
+    copies = [
+        pltpu.make_async_copy(pieces.at[y], out.at[:, :, LANES * y : LANES * (y + 1)], sems.at[y])
+        for y in range(pieces.shape[0])
+    ]
+    for copy in copies:
+        copy.start()
+    for copy in copies:
+        copy.wait()
 
 
 def float_like(*shape):
@@ -312,46 +365,62 @@
     message = near(NICE * NSUB + 2 * levels, cols)
 
 
-    planes, inner, outer = pl.pallas_call(
-        pack_kernel,
-        out_shape=[near(NICE, rows, cols), message, message],
-        in_specs=[vmem()] * 9,
+    sources = (warm, salt, ocean, wind, ice, cover, volume, wet, icy)
+    half = lambda a: a.shape[:-2] + (rows // 2, cols)
+    anywhere = pl.BlockSpec(memory_space=pl.ANY)
+    outer = pl.pallas_call(
+        outer_kernel,
+        out_shape=message,
+        in_specs=[anywhere] * len(sources),
+        out_specs=vmem(),
+        scratch_shapes=[pltpu.VMEM(half(a), a.dtype) for a in sources[2:]]
+        + [pltpu.SemaphoreType.DMA((len(sources) - 2,)), pltpu.SemaphoreType.DMA((2,))],
+        name="outer_pack",
+    )(*sources[2:], warm, salt)
+    outer = lax.ppermute(outer, "grp", outer_pairs)
+    blocks = home.shape[1]
+    own = near(rows, LANES)
+    planes, inner, low, high, sea, chosen = pl.pallas_call(
+        inner_kernel,
+        out_shape=[
+            near(NICE, rows, cols), message, own, own, near(rows, cols), near(blocks * blocks, 8, LANES),
+        ],
+        in_specs=[vmem()] * 9 + [pl.BlockSpec(memory_space=pltpu.SMEM)],
+        out_specs=[vmem()] * 6,
+        name="inner_pack",
+    )(*sources, home)
+    inner = lax.ppermute(inner, "grp", inner_pairs)
+
+    edge, first, second = pl.pallas_call(
+        edge_kernel,
+        out_shape=[near(NICE, 2 * NSUB, cols), tile, tile],
+        in_specs=[vmem()] * 4,
         out_specs=[vmem()] * 3,
-        name="pack",
-    )(warm, salt, ocean, wind, ice, cover, volume, wet, icy)
-    outer = lax.ppermute(outer, "grp", outer_pairs)
-    inner = lax.ppermute(inner, "grp", inner_pairs)
-
-    edge, first, second = pl.pallas_call(
-        columns_kernel,
-        out_shape=[near(NICE, 2 * NSUB, cols), tile, tile],
-        in_specs=[vmem()] * 6,
-        out_specs=[vmem()] * 3,
-        name="columns",
-    )(warm, salt, wet, *held(planes, inner, outer))
+        name="edge",
+    )(*held(inner, outer, low, high))
+    second = lax.ppermute(second, "gy", second_pairs)
     first = lax.ppermute(first, "gy", first_pairs)
-    second = lax.ppermute(second, "gy", second_pairs)
 
     velocity, picked = pl.pallas_call(
         ice_kernel,
-        out_shape=[float_like(2, rows, cols), float_like(gy, 5, rows, LANES)],
-        in_specs=[vmem()] * 5 + [pl.BlockSpec(memory_space=pltpu.SMEM)],
+        out_shape=[near(2, rows, cols), float_like(gy, 5, rows, LANES)],
+        in_specs=[vmem()] * 6,
         out_specs=[vmem()] * 2,
         name="ice",
-    )(*held(planes, edge, first, second), wet, home)
+    )(*held(planes, edge, first, second, sea, chosen))
     owned = lax.all_to_all(picked, "gy", split_axis=0, concat_axis=0, tiled=True)
 
     steps = 4
     block = pl.BlockSpec((levels // steps, rows, cols), lambda i: (i, 0, 0))
-    warm_out, salt_out = pl.pallas_call(
+    warm_out, salt_out, velocity = pl.pallas_call(
         tracer_kernel,
         grid=(steps,),
         in_specs=[
-            vmem(), vmem(), spec(wet.shape), spec(icy.shape), spec(cover.shape), spec(volume.shape),
-            vmem(), vmem(), vmem(), vmem(),
+            vmem(), vmem(), vmem(), spec(icy.shape), spec(cover.shape), spec(volume.shape),
+            vmem(), vmem(), vmem(), vmem(), vmem(),
         ],
-        out_specs=[block, block],
-        out_shape=[float_like(*warm.shape), float_like(*salt.shape)],
+        out_specs=[block, block, spec(ocean.shape)],
+        out_shape=[float_like(*warm.shape), float_like(*salt.shape), float_like(*ocean.shape)],
         scratch_shapes=[
             pltpu.VMEM((5, rows, cols), jnp.float32),
             pltpu.VMEM((rows, LANES), jnp.float32),
@@ -360,13 +429,14 @@
             pltpu.VMEM((2 * levels, cols), jnp.float32),
         ],
         name="tracers",
-    )(warm, salt, wet, icy, cover, volume, *held(first, second, inner, outer))
+    )(warm, salt, *held(sea), icy, cover, volume, *held(first, second, inner, outer, velocity))
 
     patch = pl.pallas_call(
         place_kernel,
         out_shape=float_like(5, rows, cols),
         in_specs=[vmem()],
-        out_specs=vmem(),
+        out_specs=anywhere,
+        scratch_shapes=[pltpu.SemaphoreType.DMA((gy,))],
         name="place",
     )(*held(owned))
     return warm_out, salt_out, velocity, patch

time: 53.2 us -> 48.1 us (0.904)
  waiting for transfers between devices: 8.52 us -> 6.09 us
  starting transfers between devices: 32.6 us -> 31 us
  Pallas kernels: 10.9 us -> 9.93 us
    ppermute x1, waiting for transfers between devices: 4.99 us -> 1.01 us  [per_device(): outer = lax.ppermute(outer, 'grp', outer_pairs)]
    ppermute x1, starting transfers between devices: 3.26 us -> 1.92 us  [per_device(): second = lax.ppermute(second, 'gy', second_pairs)]
    ppermute x1, starting transfers between devices: 2.13 us -> 3.26 us  [per_device(): first = lax.ppermute(first, 'gy', first_pairs)]
    ppermute x1, waiting for transfers between devices: 2.14 us -> 3.26 us  [per_device(): second = lax.ppermute(second, 'gy', second_pairs)]
    pallas_call x4 -> x5, Pallas kernels: 10.2 us -> 9.24 us  [the longest x1 4.35 us: per_device(): pl.pallas_call(tracer_kernel, grid=(steps,), in_specs=[vmem(), vmem(), vm...]
    all_to_all x1, starting transfers between devices: 4.08 us -> 3.34 us  [per_device(): lax.all_to_all(picked, 'gy', split_axis=0, concat_axis=0, tiled=True)]
    ppermute x1, starting transfers between devices: 21.2 us -> 20.6 us  [per_device(): outer = lax.ppermute(outer, 'grp', outer_pairs)]
  transfers between devices with their start and end apart: 5 -> 5, of which waited for: 4 -> 5; matrix products, arithmetic and copies ran while one was open for 0% -> 0% of each run, Pallas kernels for 8% -> 13%
where the time goes in v2:
time: 48.1 us; the launch traced here: 47.7 us
  starting transfers between devices  31 us (64%)
  Pallas kernels  9.93 us (21%)
  waiting for transfers between devices  6.09 us (13%)
  between operations  0.69 us (1%)
    ppermute x1, starting transfers between devices, per_device(): outer = lax.ppermute(outer, 'grp', outer_pairs)  20.6 us
    pallas_call x1, Pallas kernels, per_device(): pl.pallas_call(tracer_kernel, grid=(steps,), in_specs=[vmem(), vmem(), vm...  4.35 us
    all_to_all x1, starting transfers between devices, per_device(): lax.all_to_all(picked, 'gy', split_axis=0, concat_axis=0, tiled=True)  3.34 us
    ppermute x1, waiting for transfers between devices, per_device(): second = lax.ppermute(second, 'gy', second_pairs)  3.26 us
    ppermute x1, starting transfers between devices, per_device(): first = lax.ppermute(first, 'gy', first_pairs)  3.26 us
    pallas_call x1, Pallas kernels, per_device(): pl.pallas_call(inner_kernel, out_shape=[near(NICE, rows, cols), message,...  1.98 us
    ppermute x1, starting transfers between devices, per_device(): inner = lax.ppermute(inner, 'grp', inner_pairs)  1.92 us
    ppermute x1, starting transfers between devices, per_device(): second = lax.ppermute(second, 'gy', second_pairs)  1.92 us
  transfers between devices with their start and end apart: 5, of which 5 were waited for; matrix products, arithmetic and copies ran while one was open for 0% of the time, Pallas kernels for 13%

profile of v2, /device:TPU:8, one launch (start us, length us, event | category | flops | bytes accessed | tf_op | source)
XLA Modules:
  0.0 47.7 jit_solution(4210177862330027282)
XLA Ops:
  0.6 1.1 %outer_pack.1 = f32[96,512]{1,0:T(8,128)S(1)} custom-call(f32[2,16,512]{2,1,0:T(8,128)} %refs_0_.1, f32[2,16,512]{2,1,0:T(8,128)} %refs_1_.1, f32[5,16,512]{2,1,0:T(8,128)} %refs_2_.1, f32[5,16,512]{2,1,0:T(8,128)} %cover.3, f32[5,16,512]{2,1,0:T(8,128)} %volume.3, s32[16,512]{1,0:T(8,128)} %refs_5_.1, s32[16,512]{1,0:T(8,128)} %icy.3, f32[24,16,512]{2,1,0:T(8,128)} %warm.3, ...), custom_call_target="tpu_custom_call" | custom-call | tf_op jit(solution)/shard_map/outer_pack/pallas_call | solution.py:371
  1.8 20.6 %collective-permute-start.1 = (f32[96,512]{1,0:T(8,128)S(1)}, f32[96,512]{1,0:T(8,128)S(1)}, u32[]{:S(2)}, u32[]{:S(2)}) collective-permute-start(f32[96,512]{1,0:T(8,128)S(1)} %outer_pack.1), channel_id=1, source_target_pairs={{4,8},{8,4},{12,16},{16,12},{20,24},{24,20},{28,32},{32,28},{36,40... | collective-permute-start | bytes 589832 | tf_op jit(solution)/shard_map/ppermute | solution.py:380
  22.4 2.0 %inner_pack.1 = (f32[12,16,512]{2,1,0:T(8,128)S(1)}, f32[96,512]{1,0:T(8,128)S(1)}, f32[16,128]{1,0:T(8,128)S(1)}, f32[16,128]{1,0:T(8,128)S(1)}, f32[16,512]{1,0:T(8,128)S(1)}, /*index=5*/f32[16,8,128]{2,1,0:T(8,128)S(1)}) custom-call(f32[24,16,512]{2,1,0:T(8,128)} %warm.3, f32[24,16,512]{2,1,0:T(8,128)} %salt.3, f32[2,16,512]{2,1,0:T(8,128)} %refs_0_.1, ...), custom_call_target="tpu_custom_call" | custom-call | tf_op jit(solution)/shard_map/inner_pack/pallas_call | solution.py:383
  24.4 1.9 %collective-permute-start = (f32[96,512]{1,0:T(8,128)S(1)}, f32[96,512]{1,0:T(8,128)S(1)}, u32[]{:S(2)}, u32[]{:S(2)}) collective-permute-start(f32[96,512]{1,0:T(8,128)S(1)} %get-tuple-element.19), channel_id=1, source_target_pairs={{0,4},{4,0},{8,12},{12,8},{16,20},{20,16},{24,28},{28,24},{32,36},... | collective-permute-start | bytes 589832 | tf_op jit(solution)/shard_map/ppermute | solution.py:392
  26.3 1.0 %collective-permute-done.1.outer = f32[96,512]{1,0:T(8,128)S(1)} collective-permute-done((f32[96,512]{1,0:T(8,128)S(1)}, f32[96,512]{1,0:T(8,128)S(1)}, u32[]{:S(2)}, u32[]{:S(2)}) %collective-permute-start.1) | collective-permute-done | bytes 196640 | tf_op jit(solution)/shard_map/ppermute | solution.py:380
  27.3 0.4 collective-permute-done.inner
  27.7 0.1 edge.1
  27.8 3.3 %collective-permute-start.2 = (f32[24,128]{1,0:T(8,128)S(1)}, f32[24,128]{1,0:T(8,128)S(1)}, u32[]{:S(2)}, u32[]{:S(2)}) collective-permute-start(f32[24,128]{1,0:T(8,128)S(1)} %get-tuple-element.22), channel_id=1, source_target_pairs={{0,1},{1,0},{2,3},{3,2},{4,5},{5,4},{6,7},{7,6},{8,9},{9,8},{10,11... | collective-permute-start | bytes 36872 | tf_op jit(solution)/shard_map/ppermute | solution.py:402
  31.1 1.9 %collective-permute-start.3 = (f32[24,128]{1,0:T(8,128)S(1)}, f32[24,128]{1,0:T(8,128)S(1)}, u32[]{:S(2)}, u32[]{:S(2)}) collective-permute-start(f32[24,128]{1,0:T(8,128)S(1)} %get-tuple-element.23), channel_id=1, source_target_pairs={{1,2},{2,1},{5,6},{6,5},{9,10},{10,9},{13,14},{14,13},{17,18},{18,... | collective-permute-start | bytes 36872 | tf_op jit(solution)/shard_map/ppermute | solution.py:401
  33.0 0.4 collective-permute-done.2.first
  33.4 3.3 %collective-permute-done.3.second = f32[24,128]{1,0:T(8,128)S(1)} collective-permute-done((f32[24,128]{1,0:T(8,128)S(1)}, f32[24,128]{1,0:T(8,128)S(1)}, u32[]{:S(2)}, u32[]{:S(2)}) %collective-permute-start.3) | collective-permute-done | bytes 12320 | tf_op jit(solution)/shard_map/ppermute | solution.py:401
  36.7 1.6 %ice.3 = (f32[2,16,512]{2,1,0:T(8,128)S(1)}, f32[4,5,16,128]{3,2,1,0:T(8,128)}) custom-call(f32[12,16,512]{2,1,0:T(8,128)S(1)} %get-tuple-element.24.planes, f32[12,8,512]{2,1,0:T(8,128)S(1)} %get-tuple-element.25.edge, f32[24,128]{1,0:T(8,128)S(1)} %collective-permute-done.2.first, f32[24,128]{1,0:T(8,128)S(1)} %collective-permute-done.3.second, ...), custom_call_target="tpu_custom_call" | custom-call | tf_op jit(solution)/shard_map/ice/pallas_call | solution.py:404
  38.3 3.3 %all-to-all-start = ((f32[4,5,16,128]{3,2,1,0:T(8,128)}), f32[4,5,16,128]{3,2,1,0:T(8,128)S(1)}, u32[]{:S(2)}, u32[]{:S(2)}) async-start(f32[4,5,16,128]{3,2,1,0:T(8,128)} %get-tuple-element.31), calls=%async_computation | async-start | bytes 327680 | tf_op jit(solution)/shard_map/all_to_all | solution.py:411
  41.7 4.4 %tracers.1 = (f32[24,16,512]{2,1,0:T(8,128)}, f32[24,16,512]{2,1,0:T(8,128)}, f32[2,16,512]{2,1,0:T(8,128)}) custom-call(f32[24,16,512]{2,1,0:T(8,128)} %warm.3, f32[24,16,512]{2,1,0:T(8,128)} %salt.3, f32[16,512]{1,0:T(8,128)S(1)} %get-tuple-element.18.sea.sea_in, s32[16,512]{1,0:T(8,128)} %icy.3, f32[5,16,512]{2,1,0:T(8,128)} %cover.3, ...), custom_call_target="tpu_custom_call" | custom-call | tf_op jit(solution)/shard_map/tracers/pallas_call | solution.py:415
  46.0 1.0 %all-to-all-done.pieces = f32[4,5,16,128]{3,2,1,0:T(8,128)S(1)} async-done(((f32[4,5,16,128]{3,2,1,0:T(8,128)}), f32[4,5,16,128]{3,2,1,0:T(8,128)S(1)}, u32[]{:S(2)}, u32[]{:S(2)}) %all-to-all-start) | async-done | bytes 163872 | tf_op jit(solution)/shard_map/all_to_all | solution.py:411
  47.0 0.7 %place.1 = f32[5,16,512]{2,1,0:T(8,128)} custom-call(f32[4,5,16,128]{3,2,1,0:T(8,128)S(1)} %all-to-all-done.pieces), custom_call_target="tpu_custom_call" | custom-call | tf_op jit(solution)/shard_map/place/pallas_call | solution.py:434
Async XLA Ops:
  1.8 25.5 %collective-permute-start.1 = (f32[96,512]{1,0:T(8,128)S(1)}, f32[96,512]{1,0:T(8,128)S(1)}, u32[]{:S(2)}, u32[]{:S(2)}) collective-permute-start(f32[96,512]{1,0:T(8,128)S(1)} %outer_pack.1), channel_id=1, source_target_pairs={{4,8},{8,4},{12,16},{16,12},{20,24},{24,20},{28,32},{32,28},{36,40... | collective-permute-start | bytes 589832 | tf_op jit(solution)/shard_map/ppermute | solution.py:380
  24.4 3.3 %collective-permute-start = (f32[96,512]{1,0:T(8,128)S(1)}, f32[96,512]{1,0:T(8,128)S(1)}, u32[]{:S(2)}, u32[]{:S(2)}) collective-permute-start(f32[96,512]{1,0:T(8,128)S(1)} %get-tuple-element.19), channel_id=1, source_target_pairs={{0,4},{4,0},{8,12},{12,8},{16,20},{20,16},{24,28},{28,24},{32,36},... | collective-permute-start | bytes 589832 | tf_op jit(solution)/shard_map/ppermute | solution.py:392
  27.8 5.6 %collective-permute-start.2 = (f32[24,128]{1,0:T(8,128)S(1)}, f32[24,128]{1,0:T(8,128)S(1)}, u32[]{:S(2)}, u32[]{:S(2)}) collective-permute-start(f32[24,128]{1,0:T(8,128)S(1)} %get-tuple-element.22), channel_id=1, source_target_pairs={{0,1},{1,0},{2,3},{3,2},{4,5},{5,4},{6,7},{7,6},{8,9},{9,8},{10,11... | collective-permute-start | bytes 36872 | tf_op jit(solution)/shard_map/ppermute | solution.py:402
  31.1 5.6 %collective-permute-start.3 = (f32[24,128]{1,0:T(8,128)S(1)}, f32[24,128]{1,0:T(8,128)S(1)}, u32[]{:S(2)}, u32[]{:S(2)}) collective-permute-start(f32[24,128]{1,0:T(8,128)S(1)} %get-tuple-element.23), channel_id=1, source_target_pairs={{1,2},{2,1},{5,6},{6,5},{9,10},{10,9},{13,14},{14,13},{17,18},{18,... | collective-permute-start | bytes 36872 | tf_op jit(solution)/shard_map/ppermute | solution.py:401
  38.3 8.7 %all-to-all-start = ((f32[4,5,16,128]{3,2,1,0:T(8,128)}), f32[4,5,16,128]{3,2,1,0:T(8,128)S(1)}, u32[]{:S(2)}, u32[]{:S(2)}) async-start(f32[4,5,16,128]{3,2,1,0:T(8,128)} %get-tuple-element.31), calls=%async_computation | async-start | bytes 327680 | tf_op jit(solution)/shard_map/all_to_all | solution.py:411

commit v3 on v2

--- a/solution.py
+++ b/solution.py
@@ -25,7 +25,8 @@
 NICE = 12
 WET_ROW = WX
 LANES = 128
-TRACER_LANE = NICE * NSUB
+REACH = 2 * NSUB
+FLOW_LANE, HOME_LANE = 32, 64
 
 
 def even(axis):
@@ -85,20 +86,17 @@
 
 
 def gathered(source, count):
-    cols = source.shape[2]
     lane = lax.broadcasted_iota(jnp.int32, (count, LANES), 1)
-    low = jnp.zeros((count, LANES), jnp.float32)
-    high = low
+    tile = jnp.zeros((count, LANES), jnp.float32)
     for p in range(NICE):
-        here = (lane >= NSUB * p) & (lane < NSUB * (p + 1))
-        low = jnp.where(here, pltpu.roll(source[p, :, :LANES], NSUB * p, 1), low)
-        high = jnp.where(here, pltpu.roll(source[p, :, cols - LANES :], NSUB * (p + 1), 1), high)
-    return lane, low, high
+        here = (lane >= REACH * p) & (lane < REACH * (p + 1))
+        tile = jnp.where(here, pltpu.roll(source[p, :, :LANES], REACH * p, 1), tile)
+    return tile
 
 
 def inner_kernel(
     warm, salt, ocean, wind, ice, cover, volume, wet, icy, home,
-    planes, inner, low_out, high_out, sea, chosen,
+    planes, inner, own, down, up, sea, chosen,
 ):
     levels, rows, cols = warm.shape
     for k in range(5):
@@ -133,21 +131,24 @@
     def _():
         message(0, NSUB - 1, 0)
 
-    lane, low, high = gathered(planes, rows)
+    own[...] = gathered(planes, rows)
+    lane = lax.broadcasted_iota(jnp.int32, (rows, LANES), 1)
+    first_home = home[0, 0].astype(jnp.float32)
+    low = jnp.where((lane >= HOME_LANE) & (lane < HOME_LANE + NSUB), first_home, 0.0)
+    high = jnp.zeros((rows, LANES), jnp.float32)
     for p in range(2 * levels + 1):
         if p < 2 * levels:
             field = warm[p] if p < levels else salt[p - levels]
         else:
             field = sea[...]
-        at = TRACER_LANE + p
-        low = jnp.where(lane == at, pltpu.roll(field[:, :LANES], at, 1), low)
-        high = jnp.where(lane == at, pltpu.roll(field[:, cols - LANES :], at + 1, 1), high)
-    low_out[...] = low
-    high_out[...] = high
-
-
-def edge_kernel(inner, outer, low, high, edge, first, second):
-    rows = low.shape[0]
+        low = jnp.where(lane == p, pltpu.roll(field[:, :LANES], p, 1), low)
+        high = jnp.where(lane == p, pltpu.roll(field[:, cols - LANES :], p + 1, 1), high)
+    down[...] = low
+    up[...] = high
+
+
+def edge_kernel(inner, outer, own, tracer, edge, down):
+    rows = own.shape[0]
 
     def place(east, west):
         for p in range(NICE):
@@ -162,40 +163,30 @@
     def _():
         place(outer, inner)
 
-    _, low_edge, high_edge = gathered(edge, 2 * NSUB)
-    north_first = even("gy")
-    first[:rows, :] = jnp.where(north_first, high[...], low[...])
-    first[rows:, :] = jnp.where(north_first, high_edge, low_edge)
-    second[:rows, :] = jnp.where(north_first, low[...], high[...])
-    second[rows:, :] = jnp.where(north_first, low_edge, high_edge)
-
-
-def sides(first, second):
-    north_first = even("gy")
-    one, two = first[...], second[...]
-    return jnp.where(north_first, two, one), jnp.where(north_first, one, two)
-
-
-def columns_of(low, high, p):
-    lane = lax.broadcasted_iota(jnp.int32, low.shape, 1)
-    above = high if p == 0 else pltpu.roll(high, LANES - NSUB * p, 1)
-    below = pltpu.roll(low, LANES - NSUB * (p + 1), 1)
-    return jnp.where(lane < NSUB, above, jnp.where(lane >= LANES - NSUB, below, 0.0))
+    tall = rows + 2 * NSUB
+    down[:rows, :] = own[...]
+    down[rows:tall, :] = gathered(edge, 2 * NSUB)
+    down[tall:, :] = tracer[...]
+
+
+def columns_of(tile, p):
+    lane = lax.broadcasted_iota(jnp.int32, tile.shape, 1)
+    return jnp.where(lane < REACH, tile if p == 0 else pltpu.roll(tile, LANES - REACH * p, 1), 0.0)
 
 
 def root(square):
     return square * lax.rsqrt(square)
 
 
-def ice_kernel(planes, edge, first, second, sea, chosen, velocity, picked):
+def ice_kernel(planes, edge, down, sea, chosen, velocity, picked):
     rows, cols = sea.shape
     pieces = cols // LANES
     tall = rows + 2 * NSUB
     broad = cols + LANES
-    low, high = sides(first, second)
+    tile = down[:tall, :]
     wide = [
         jnp.concatenate(
-            [jnp.concatenate([planes[p], edge[p]], axis=0), columns_of(low, high, p)], axis=1
+            [jnp.concatenate([planes[p], edge[p]], axis=0), columns_of(tile, p)], axis=1
         )
         for p in range(NICE)
     ]
@@ -230,14 +221,29 @@
             scale * (mass * u + force_u + wide[WX] + coef * ocean_u + turn * v),
             scale * (mass * v + force_v + wide[WY] + coef * ocean_v - turn * u),
         )
-    own = lambda f: f[:rows, :cols]
-    u, v, ocean_u, ocean_v = own(u), own(v), own(ocean_u), own(ocean_v)
+    own = lambda f: f[:rows, :]
+    u, v, s1, s2, s12, ocean_u, ocean_v = (own(f) for f in (u, v, s1, s2, s12, ocean_u, ocean_v))
     coef = own(area) * root((ocean_u - u) ** 2 + (ocean_v - v) ** 2 + SPEED_FLOOR)
     drag = (STRESS_SCALE * own(mask)) * coef
-    velocity[0] = sea[...] * (ocean_u + drag * (u - ocean_u))
-    velocity[1] = sea[...] * (ocean_v + drag * (v - ocean_v))
+    flow = (ocean_u + drag * (u - ocean_u), ocean_v + drag * (v - ocean_v))
+    lane = lax.broadcasted_iota(jnp.int32, (rows, LANES), 1)
+    strip = jnp.zeros((rows, LANES), jnp.float32)
+    for k, f in enumerate((u, v, s1, s2, s12)):
+        at = NSUB * k
+        moved = pltpu.roll(f[:, cols:], at, 1) if at else f[:, cols:]
+        strip = jnp.where((lane >= at) & (lane < at + NSUB), moved, strip)
+    for k, f in enumerate(flow):
+        velocity[k] = sea[...] * f[:, :cols]
+        at = FLOW_LANE + NSUB * k
+        strip = jnp.where((lane >= at) & (lane < at + NSUB), pltpu.roll(f[:, cols:], at, 1), strip)
+    next_home = down[tall:, :]
+    inland = lax.axis_index("gy") < picked.shape[0] - 1
+    flagged = (lane >= HOME_LANE) & (lane < HOME_LANE + NSUB)
+    for owner in range(pieces):
+        flag = jnp.where(inland, jnp.where(next_home == float(owner), 1.0, 0.0), 0.0)
+        picked[owner, 5] = jnp.where(flagged, flag, strip)
     here = [jnp.concatenate([chosen[k]] * (rows // 8), axis=0) > 0.5 for k in range(pieces * pieces)]
-    for k, f in enumerate((u, v, own(s1), own(s2), own(s12))):
+    for k, f in enumerate((u, v, s1, s2, s12)):
         blocks = [f[:, LANES * b : LANES * (b + 1)] for b in range(pieces)]
         for owner in range(pieces):
             value = jnp.zeros_like(blocks[0])
@@ -247,14 +253,13 @@
 
 
 def tracer_kernel(
-    warm, salt, sea_in, icy, cover, volume, first, second, inner, outer, flow,
-    warm_out, salt_out, flow_out, coef, cut_low, cut_high, gain, rise,
+    warm, salt, sea_in, icy, cover, volume, up, down, inner, outer,
+    warm_out, salt_out, coef, cut_low, cut_high, gain, rise,
 ):
     step = pl.program_id(0)
     levels, rows, cols = warm.shape
     count = warm_out.shape[0]
-    low, high = sides(first, second)
-    low, high = low[:rows], high[:rows]
+    low, high = up[...], down[rows + 2 * NSUB :, :]
     top = NICE * NSUB
 
     @pl.when(step == 0)
@@ -262,14 +267,13 @@
         lane = lax.broadcasted_iota(jnp.int32, (rows, cols), 1)
         row = lax.broadcasted_iota(jnp.int32, (rows, cols), 0)
         short = lax.broadcasted_iota(jnp.int32, (rows, LANES), 1)
-        flow_out[...] = flow[...]
         sea = sea_in[...]
         mine = DIFFUSIVITY * sea
         east = jnp.where(row < rows - 1, mine * pltpu.roll(sea, rows - 1, 0), 0.0)
         west = jnp.where(row > 0, mine * pltpu.roll(sea, 1, 0), 0.0)
         north = jnp.where(lane < cols - 1, mine * pltpu.roll(sea, cols - 1, 1), 0.0)
         south = jnp.where(lane > 0, mine * pltpu.roll(sea, 1, 1), 0.0)
-        at = TRACER_LANE + 2 * levels
+        at = 2 * levels
         edge_low = jnp.where(short == 0, mine[:, :LANES] * pltpu.roll(low, LANES - at, 1), 0.0)
         edge_high = jnp.where(
             short == LANES - 1,
@@ -311,7 +315,7 @@
                 + coef[4] * pltpu.roll(f, 1, 1)
             )
             plane = part * levels + level
-            at = TRACER_LANE + plane
+            at = plane
             out[k, :, :LANES] += cut_low[...] * pltpu.roll(low, LANES - at, 1)
             out[k, :, cols - LANES :] += cut_high[...] * pltpu.roll(high, LANES - 1 - at, 1)
             out[k, rows - 1 :, :] += rise[pl.ds(plane, 1), :]
@@ -326,15 +330,31 @@
         warm_out[0] -= WARMTH_FACTOR * sea_in[...] * heat
 
 
-def place_kernel(pieces, out, sems):
-    copies = [
-        pltpu.make_async_copy(pieces.at[y], out.at[:, :, LANES * y : LANES * (y + 1)], sems.at[y])
-        for y in range(pieces.shape[0])
-    ]
-    for copy in copies:
-        copy.start()
-    for copy in copies:
-        copy.wait()
+def place_kernel(owned, velocity, sea, patch_out, velocity_out, patch, shifted, sems):
+    tiles, _, rows, _ = owned.shape
+    lane = lax.broadcasted_iota(jnp.int32, (rows, LANES), 1)
+    for y in range(tiles):
+        for k in range(5):
+            value = owned[y, k]
+            if y:
+                strip = owned[y - 1, 5]
+                sent = (lane < NSUB) & (pltpu.roll(strip, LANES - HOME_LANE, 1) > 0.5)
+                moved = pltpu.roll(strip, LANES - NSUB * k, 1) if k else strip
+                value = jnp.where(sent, moved, value)
+            patch[k, :, LANES * y : LANES * (y + 1)] = value
+    patch_copy = pltpu.make_async_copy(patch, patch_out, sems.at[0])
+    patch_copy.start()
+    at = lax.axis_index("gy")
+    strip = owned[jnp.maximum(at - 1, 0), 5]
+    for k in range(2):
+        value = pltpu.roll(strip, LANES - FLOW_LANE - NSUB * k, 1)
+        low = jnp.where(at > 0, lane, LANES) < NSUB
+        shifted[k] = velocity[k]
+        shifted[k, :, :LANES] = jnp.where(low, sea[:, :LANES] * value, velocity[k, :, :LANES])
+    velocity_copy = pltpu.make_async_copy(shifted, velocity_out, sems.at[1])
+    velocity_copy.start()
+    patch_copy.wait()
+    velocity_copy.wait()
 
 
 def float_like(*shape):
@@ -358,10 +378,10 @@
     swap = lambda pairs: [p for i, j in pairs for p in ((i, j), (j, i))]
     inner_pairs = swap([(i, i + 1) for i in range(0, grp, 2)])
     outer_pairs = swap([(i, (i + 1) % grp) for i in range(1, grp, 2)])
-    first_pairs = swap([(i, i + 1) for i in range(0, gy, 2)])
-    second_pairs = swap([(i, i + 1) for i in range(1, gy - 1, 2)])
+    up_pairs = [(i, i + 1) for i in range(gy - 1)]
+    down_pairs = [(j, i) for i, j in up_pairs]
     tall = rows + 2 * NSUB
-    tile = near(tall, LANES)
+    tile = near(rows, LANES)
     message = near(NICE * NSUB + 2 * levels, cols)
 
 
@@ -379,48 +399,47 @@
     )(*sources[2:], warm, salt)
     outer = lax.ppermute(outer, "grp", outer_pairs)
     blocks = home.shape[1]
-    own = near(rows, LANES)
-    planes, inner, low, high, sea, chosen = pl.pallas_call(
+    planes, inner, own, down, up, sea, chosen = pl.pallas_call(
         inner_kernel,
         out_shape=[
-            near(NICE, rows, cols), message, own, own, near(rows, cols), near(blocks * blocks, 8, LANES),
+            near(NICE, rows, cols), message, tile, tile, tile, near(rows, cols), near(blocks * blocks, 8, LANES),
         ],
         in_specs=[vmem()] * 9 + [pl.BlockSpec(memory_space=pltpu.SMEM)],
-        out_specs=[vmem()] * 6,
+        out_specs=[vmem()] * 7,
         name="inner_pack",
     )(*sources, home)
     inner = lax.ppermute(inner, "grp", inner_pairs)
-
-    edge, first, second = pl.pallas_call(
+    up = lax.ppermute(up, "gy", up_pairs)
+
+    edge, down = pl.pallas_call(
         edge_kernel,
-        out_shape=[near(NICE, 2 * NSUB, cols), tile, tile],
+        out_shape=[near(NICE, 2 * NSUB, cols), near(tall + rows, LANES)],
         in_specs=[vmem()] * 4,
-        out_specs=[vmem()] * 3,
+        out_specs=[vmem()] * 2,
         name="edge",
-    )(*held(inner, outer, low, high))
-    second = lax.ppermute(second, "gy", second_pairs)
-    first = lax.ppermute(first, "gy", first_pairs)
+    )(*held(inner, outer, own, down))
+    down = lax.ppermute(down, "gy", down_pairs)
 
     velocity, picked = pl.pallas_call(
         ice_kernel,
-        out_shape=[near(2, rows, cols), float_like(gy, 5, rows, LANES)],
-        in_specs=[vmem()] * 6,
+        out_shape=[near(2, rows, cols), float_like(gy, 6, rows, LANES)],
+        in_specs=[vmem()] * 5,
         out_specs=[vmem()] * 2,
         name="ice",
-    )(*held(planes, edge, first, second, sea, chosen))
+    )(*held(planes, edge, down, sea, chosen))
     owned = lax.all_to_all(picked, "gy", split_axis=0, concat_axis=0, tiled=True)
 
     steps = 4
     block = pl.BlockSpec((levels // steps, rows, cols), lambda i: (i, 0, 0))
-    warm_out, salt_out, velocity = pl.pallas_call(
+    warm_out, salt_out = pl.pallas_call(
         tracer_kernel,
         grid=(steps,),
         in_specs=[
             vmem(), vmem(), vmem(), spec(icy.shape), spec(cover.shape), spec(volume.shape),
-            vmem(), vmem(), vmem(), vmem(), vmem(),
+            vmem(), vmem(), vmem(), vmem(),
         ],
-        out_specs=[block, block, spec(ocean.shape)],
-        out_shape=[float_like(*warm.shape), float_like(*salt.shape), float_like(*ocean.shape)],
+        out_specs=[block, block],
+        out_shape=[float_like(*warm.shape), float_like(*salt.shape)],
         scratch_shapes=[
             pltpu.VMEM((5, rows, cols), jnp.float32),
             pltpu.VMEM((rows, LANES), jnp.float32),
@@ -429,16 +448,20 @@
             pltpu.VMEM((2 * levels, cols), jnp.float32),
         ],
         name="tracers",
-    )(warm, salt, *held(sea), icy, cover, volume, *held(first, second, inner, outer, velocity))
-
-    patch = pl.pallas_call(
+    )(warm, salt, *held(sea), icy, cover, volume, *held(up, down, inner, outer))
+
+    patch, velocity = pl.pallas_call(
         place_kernel,
-        out_shape=float_like(5, rows, cols),
-        in_specs=[vmem()],
-        out_specs=anywhere,
-        scratch_shapes=[pltpu.SemaphoreType.DMA((gy,))],
+        out_shape=[float_like(5, rows, cols), float_like(2, rows, cols)],
+        in_specs=[vmem()] * 3,
+        out_specs=[anywhere] * 2,
+        scratch_shapes=[
+            pltpu.VMEM((5, rows, cols), jnp.float32),
+            pltpu.VMEM((2, rows, cols), jnp.float32),
+            pltpu.SemaphoreType.DMA((2,)),
+        ],
         name="place",
-    )(*held(owned))
+    )(*held(owned, velocity, sea))
     return warm_out, salt_out, velocity, patch
 
 

time: 48.1 us -> 50.9 us (1.058)
  starting transfers between devices: 31 us -> 33.8 us
    ppermute x2, starting transfers between devices: 5.18 us -> 6.62 us  [the longest x1 3.36 us: per_device(): up = lax.ppermute(up, 'gy', up_pairs)]
    all_to_all x1, starting transfers between devices: 3.34 us -> 4.68 us  [per_device(): lax.all_to_all(picked, 'gy', split_axis=0, concat_axis=0, tiled=True)]
    all_to_all x1, waiting for transfers between devices: 1.02 us -> 0.01 us  [per_device(): lax.all_to_all(picked, 'gy', split_axis=0, concat_axis=0, tiled=True)]
    ppermute x2, waiting for transfers between devices: 3.66 us -> 4.57 us  [the longest x1 2.41 us: per_device(): down = lax.ppermute(down, 'gy', down_pairs)]
  transfers between devices with their start and end apart: 5 -> 5, of which waited for: 5 -> 4; matrix products, arithmetic and copies ran while one was open for 0% -> 0% of each run, Pallas kernels for 13% -> 12%
where the time goes in v3:
time: 50.9 us; the launch traced here: 50.5 us
  starting transfers between devices  33.8 us (66%)
  Pallas kernels  10.1 us (20%)
  waiting for transfers between devices  5.98 us (12%)
  between operations  0.69 us (1%)
    ppermute x1, starting transfers between devices, per_device(): outer = lax.ppermute(outer, 'grp', outer_pairs)  20.6 us
    all_to_all x1, starting transfers between devices, per_device(): lax.all_to_all(picked, 'gy', split_axis=0, concat_axis=0, tiled=True)  4.68 us
    pallas_call x1, Pallas kernels, per_device(): pl.pallas_call(tracer_kernel, grid=(steps,), in_specs=[vmem(), vmem(), vm...  4.23 us
    ppermute x1, starting transfers between devices, per_device(): up = lax.ppermute(up, 'gy', up_pairs)  3.36 us
    ppermute x1, starting transfers between devices, per_device(): down = lax.ppermute(down, 'gy', down_pairs)  3.26 us
    ppermute x1, waiting for transfers between devices, per_device(): down = lax.ppermute(down, 'gy', down_pairs)  2.41 us
    ppermute x1, waiting for transfers between devices, per_device(): up = lax.ppermute(up, 'gy', up_pairs)  2.16 us
    pallas_call x1, Pallas kernels, per_device(): pl.pallas_call(inner_kernel, out_shape=[near(NICE, rows, cols), message,...  2 us
  transfers between devices with their start and end apart: 5, of which 4 were waited for; matrix products, arithmetic and copies ran while one was open for 0% of the time, Pallas kernels for 12%

profile of v3, /device:TPU:8, one launch (start us, length us, event | category | flops | bytes accessed | tf_op | source)
XLA Modules:
  0.0 50.5 jit_solution(11395395282431504438)
XLA Ops:
  0.6 1.1 %outer_pack.1 = f32[96,512]{1,0:T(8,128)S(1)} custom-call(f32[2,16,512]{2,1,0:T(8,128)} %refs_0_.1, f32[2,16,512]{2,1,0:T(8,128)} %refs_1_.1, f32[5,16,512]{2,1,0:T(8,128)} %refs_2_.1, f32[5,16,512]{2,1,0:T(8,128)} %cover.3, f32[5,16,512]{2,1,0:T(8,128)} %volume.3, s32[16,512]{1,0:T(8,128)} %refs_5_.1, s32[16,512]{1,0:T(8,128)} %icy.3, f32[24,16,512]{2,1,0:T(8,128)} %warm.3, ...), custom_call_target="tpu_custom_call" | custom-call | tf_op jit(solution)/shard_map/outer_pack/pallas_call | solution.py:391
  1.8 20.6 %collective-permute-start.2 = (f32[96,512]{1,0:T(8,128)S(1)}, f32[96,512]{1,0:T(8,128)S(1)}, u32[]{:S(2)}, u32[]{:S(2)}) collective-permute-start(f32[96,512]{1,0:T(8,128)S(1)} %outer_pack.1), channel_id=1, source_target_pairs={{4,8},{8,4},{12,16},{16,12},{20,24},{24,20},{28,32},{32,28},{36,40... | collective-permute-start | bytes 589832 | tf_op jit(solution)/shard_map/ppermute | solution.py:400
  22.4 2.0 %inner_pack.1 = (f32[12,16,512]{2,1,0:T(8,128)S(1)}, f32[96,512]{1,0:T(8,128)S(1)}, f32[16,128]{1,0:T(8,128)S(1)}, f32[16,128]{1,0:T(8,128)S(1)}, f32[16,128]{1,...) custom-call(f32[24,16,512]{2,1,0:T(8,128)} %warm.3, f32[24,16,512]{2,1,0:T(8,128)} %salt.3, ...), custom_call_target="tpu_custom_call" | custom-call | tf_op jit(solution)/shard_map/inner_pack/pallas_call | solution.py:402
  24.4 1.9 %collective-permute-start.1 = (f32[96,512]{1,0:T(8,128)S(1)}, f32[96,512]{1,0:T(8,128)S(1)}, u32[]{:S(2)}, u32[]{:S(2)}) collective-permute-start(f32[96,512]{1,0:T(8,128)S(1)} %get-tuple-element.21), channel_id=1, source_target_pairs={{0,4},{4,0},{8,12},{12,8},{16,20},{20,16},{24,28},{28,24},{32,36},... | collective-permute-start | bytes 589832 | tf_op jit(solution)/shard_map/ppermute | solution.py:411
  26.3 1.0 %collective-permute-done.2.outer = f32[96,512]{1,0:T(8,128)S(1)} collective-permute-done((f32[96,512]{1,0:T(8,128)S(1)}, f32[96,512]{1,0:T(8,128)S(1)}, u32[]{:S(2)}, u32[]{:S(2)}) %collective-permute-start.2) | collective-permute-done | bytes 196640 | tf_op jit(solution)/shard_map/ppermute | solution.py:400
  27.3 0.4 collective-permute-done.1.inner
  27.7 0.1 edge.1
  27.8 3.3 %collective-permute-start.3 = (f32[40,128]{1,0:T(8,128)S(1)}, f32[40,128]{1,0:T(8,128)S(1)}, u32[]{:S(2)}, u32[]{:S(2)}) collective-permute-start(f32[40,128]{1,0:T(8,128)S(1)} %get-tuple-element.24), channel_id=1, source_target_pairs={{1,0},{2,1},{3,2},{5,4},{6,5},{7,6},{9,8},{10,9},{11,10},{13,12},{... | collective-permute-start | bytes 61448 | tf_op jit(solution)/shard_map/ppermute | solution.py:421
  31.1 2.4 %collective-permute-done.3.down = f32[40,128]{1,0:T(8,128)S(1)} collective-permute-done((f32[40,128]{1,0:T(8,128)S(1)}, f32[40,128]{1,0:T(8,128)S(1)}, u32[]{:S(2)}, u32[]{:S(2)}) %collective-permute-start.3) | collective-permute-done | bytes 20512 | tf_op jit(solution)/shard_map/ppermute | solution.py:421
  33.5 1.7 %ice.3 = (f32[2,16,512]{2,1,0:T(8,128)S(1)}, f32[4,6,16,128]{3,2,1,0:T(8,128)}) custom-call(f32[12,16,512]{2,1,0:T(8,128)S(1)} %get-tuple-element.27.planes, f32[12,8,512]{2,1,0:T(8,128)S(1)} %get-tuple-element.28.edge, f32[40,128]{1,0:T(8,128)S(1)} %collective-permute-done.3.down, f32[16,512]{1,0:T(8,128)S(1)} %get-tuple-element.19.sea_in.sea, ...), custom_call_target="tpu_custom_call" | custom-call | tf_op jit(solution)/shard_map/ice/pallas_call | solution.py:423
  35.3 4.7 %all-to-all-start = ((f32[4,6,16,128]{3,2,1,0:T(8,128)}), f32[4,6,16,128]{3,2,1,0:T(8,128)S(1)}, u32[]{:S(2)}, u32[]{:S(2)}) async-start(f32[4,6,16,128]{3,2,1,0:T(8,128)} %get-tuple-element.30), calls=%async_computation | async-start | bytes 393216 | tf_op jit(solution)/shard_map/all_to_all | solution.py:430
  39.9 3.4 %collective-permute-start = (f32[16,128]{1,0:T(8,128)S(1)}, f32[16,128]{1,0:T(8,128)S(1)}, u32[]{:S(2)}, u32[]{:S(2)}) collective-permute-start(f32[16,128]{1,0:T(8,128)S(1)} %get-tuple-element.20), channel_id=1, source_target_pairs={{0,1},{1,2},{2,3},{4,5},{5,6},{6,7},{8,9},{9,10},{10,11},{12,13},{... | collective-permute-start | bytes 24584 | tf_op jit(solution)/shard_map/ppermute | solution.py:412
  43.3 2.2 %collective-permute-done.up = f32[16,128]{1,0:T(8,128)S(1)} collective-permute-done((f32[16,128]{1,0:T(8,128)S(1)}, f32[16,128]{1,0:T(8,128)S(1)}, u32[]{:S(2)}, u32[]{:S(2)}) %collective-permute-start) | collective-permute-done | bytes 8224 | tf_op jit(solution)/shard_map/ppermute | solution.py:412
  45.5 4.2 %tracers.1 = (f32[24,16,512]{2,1,0:T(8,128)}, f32[24,16,512]{2,1,0:T(8,128)}) custom-call(f32[24,16,512]{2,1,0:T(8,128)} %warm.3, f32[24,16,512]{2,1,0:T(8,128)} %salt.3, f32[16,512]{1,0:T(8,128)S(1)} %get-tuple-element.19.sea_in.sea, s32[16,512]{1,0:T(8,128)} %icy.3, f32[5,16,512]{2,1,0:T(8,128)} %cover.3, f32[5,16,512]{2,1,0:T(8,128)} %volume.3, ...), custom_call_target="tpu_custom_call" | custom-call | tf_op jit(solution)/shard_map/tracers/pallas_call | solution.py:434
  49.7 0.0 all-to-all-done.owned
  49.7 0.8 %place.1 = (f32[5,16,512]{2,1,0:T(8,128)}, f32[2,16,512]{2,1,0:T(8,128)}) custom-call(f32[4,6,16,128]{3,2,1,0:T(8,128)S(1)} %all-to-all-done.owned, f32[2,16,512]{2,1,0:T(8,128)S(1)} %get-tuple-element.31.velocity, f32[16,512]{1,0:T(8,128)S(1)} %get-tuple-element.19.sea_in.sea), custom_call_target="tpu_custom_call" | custom-call | tf_op jit(solution)/shard_map/place/pallas_call | solution.py:453
Async XLA Ops:
  1.8 25.5 %collective-permute-start.2 = (f32[96,512]{1,0:T(8,128)S(1)}, f32[96,512]{1,0:T(8,128)S(1)}, u32[]{:S(2)}, u32[]{:S(2)}) collective-permute-start(f32[96,512]{1,0:T(8,128)S(1)} %outer_pack.1), channel_id=1, source_target_pairs={{4,8},{8,4},{12,16},{16,12},{20,24},{24,20},{28,32},{32,28},{36,40... | collective-permute-start | bytes 589832 | tf_op jit(solution)/shard_map/ppermute | solution.py:400
  24.4 3.3 %collective-permute-start.1 = (f32[96,512]{1,0:T(8,128)S(1)}, f32[96,512]{1,0:T(8,128)S(1)}, u32[]{:S(2)}, u32[]{:S(2)}) collective-permute-start(f32[96,512]{1,0:T(8,128)S(1)} %get-tuple-element.21), channel_id=1, source_target_pairs={{0,4},{4,0},{8,12},{12,8},{16,20},{20,16},{24,28},{28,24},{32,36},... | collective-permute-start | bytes 589832 | tf_op jit(solution)/shard_map/ppermute | solution.py:411
  27.8 5.7 %collective-permute-start.3 = (f32[40,128]{1,0:T(8,128)S(1)}, f32[40,128]{1,0:T(8,128)S(1)}, u32[]{:S(2)}, u32[]{:S(2)}) collective-permute-start(f32[40,128]{1,0:T(8,128)S(1)} %get-tuple-element.24), channel_id=1, source_target_pairs={{1,0},{2,1},{3,2},{5,4},{6,5},{7,6},{9,8},{10,9},{11,10},{13,12},{... | collective-permute-start | bytes 61448 | tf_op jit(solution)/shard_map/ppermute | solution.py:421
  35.3 14.5 %all-to-all-start = ((f32[4,6,16,128]{3,2,1,0:T(8,128)}), f32[4,6,16,128]{3,2,1,0:T(8,128)S(1)}, u32[]{:S(2)}, u32[]{:S(2)}) async-start(f32[4,6,16,128]{3,2,1,0:T(8,128)} %get-tuple-element.30), calls=%async_computation | async-start | bytes 393216 | tf_op jit(solution)/shard_map/all_to_all | solution.py:430
  39.9 5.5 %collective-permute-start = (f32[16,128]{1,0:T(8,128)S(1)}, f32[16,128]{1,0:T(8,128)S(1)}, u32[]{:S(2)}, u32[]{:S(2)}) collective-permute-start(f32[16,128]{1,0:T(8,128)S(1)} %get-tuple-element.20), channel_id=1, source_target_pairs={{0,1},{1,2},{2,3},{4,5},{5,6},{6,7},{8,9},{9,10},{10,11},{12,13},{... | collective-permute-start | bytes 24584 | tf_op jit(solution)/shard_map/ppermute | solution.py:412

commit v4 on v3

--- a/solution.py
+++ b/solution.py
@@ -94,55 +94,77 @@
     return tile
 
 
-def inner_kernel(
-    warm, salt, ocean, wind, ice, cover, volume, wet, icy, home,
-    planes, inner, own, down, up, sea, chosen,
-):
-    levels, rows, cols = warm.shape
-    for k in range(5):
-        planes[U + k] = ice[k]
-    planes[UO] = ocean[0]
-    planes[VO] = ocean[1]
-    planes[AREA] = sum(cover[k] for k in range(cover.shape[0]))
-    planes[THICK] = sum(volume[k] for k in range(volume.shape[0]))
-    planes[WX] = wind[0]
-    planes[WY] = wind[1]
-    planes[ICY] = icy[...].astype(jnp.float32)
-    sea[...] = wet[...].astype(jnp.float32)
+def inner_kernel(*refs):
+    warm, salt, fields = refs[0], refs[1], refs[2:9]
+    planes, inner, sea = refs[9:12]
+    tiles, sems, tile_sems = refs[12:19], refs[19], refs[20]
+    ocean, wind, ice, cover, volume, wet, icy = tiles
+    levels, rows, _ = warm.shape
+    top = NICE * NSUB
+
+    def message(row, wet_slot, edge_row):
+        lines = [
+            pltpu.make_async_copy(
+                f.at[:, edge_row, :], inner.at[top + k * levels : top + (k + 1) * levels, :], sems.at[k]
+            )
+            for k, f in enumerate((warm, salt))
+        ]
+        copies = [
+            pltpu.make_async_copy(f, held_tile, tile_sems.at[k])
+            for k, (f, held_tile) in enumerate(zip(fields, tiles))
+        ]
+        for copy in copies + lines:
+            copy.start()
+        for copy in copies:
+            copy.wait()
+        for k in range(5):
+            planes[U + k] = ice[k]
+        planes[UO] = ocean[0]
+        planes[VO] = ocean[1]
+        planes[AREA] = sum(cover[k] for k in range(cover.shape[0]))
+        planes[THICK] = sum(volume[k] for k in range(volume.shape[0]))
+        planes[WX] = wind[0]
+        planes[WY] = wind[1]
+        planes[ICY] = icy[...].astype(jnp.float32)
+        sea[...] = wet[...].astype(jnp.float32)
+        for p in range(NICE):
+            inner[NSUB * p : NSUB * (p + 1), :] = planes[p, row : row + NSUB, :]
+        at = NSUB * WET_ROW + wet_slot
+        inner[at : at + 1, :] = sea[edge_row : edge_row + 1, :]
+        for copy in lines:
+            copy.wait()
+
+    @pl.when(even("grp"))
+    def _():
+        message(rows - NSUB, 0, rows - 1)
+
+    @pl.when(jnp.logical_not(even("grp")))
+    def _():
+        message(0, NSUB - 1, 0)
+
+
+def tiles_kernel(warm_low, warm_high, salt_low, salt_high, planes, sea, home, own, down, up, chosen):
+    levels, rows, _ = warm_low.shape
+    cols = sea.shape[1]
     blocks = home.shape[1]
     for owner in range(blocks):
         for b in range(blocks):
             flag = jnp.where(home[0, b] == owner, 1.0, 0.0)
             chosen[owner * blocks + b] = jnp.full(chosen.shape[1:], flag, jnp.float32)
-
-    def message(row, wet_slot, edge_row):
-        for p in range(NICE):
-            inner[NSUB * p : NSUB * (p + 1), :] = planes[p, row : row + NSUB, :]
-        at = NSUB * WET_ROW + wet_slot
-        inner[at : at + 1, :] = sea[edge_row : edge_row + 1, :]
-        inner[NICE * NSUB : NICE * NSUB + levels, :] = warm[:, edge_row, :]
-        inner[NICE * NSUB + levels :, :] = salt[:, edge_row, :]
-
-    @pl.when(even("grp"))
-    def _():
-        message(rows - NSUB, 0, rows - 1)
-
-    @pl.when(jnp.logical_not(even("grp")))
-    def _():
-        message(0, NSUB - 1, 0)
-
     own[...] = gathered(planes, rows)
     lane = lax.broadcasted_iota(jnp.int32, (rows, LANES), 1)
     first_home = home[0, 0].astype(jnp.float32)
     low = jnp.where((lane >= HOME_LANE) & (lane < HOME_LANE + NSUB), first_home, 0.0)
     high = jnp.zeros((rows, LANES), jnp.float32)
     for p in range(2 * levels + 1):
-        if p < 2 * levels:
-            field = warm[p] if p < levels else salt[p - levels]
+        if p < levels:
+            left, right = warm_low[p], warm_high[p]
+        elif p < 2 * levels:
+            left, right = salt_low[p - levels], salt_high[p - levels]
         else:
-            field = sea[...]
-        low = jnp.where(lane == p, pltpu.roll(field[:, :LANES], p, 1), low)
-        high = jnp.where(lane == p, pltpu.roll(field[:, cols - LANES :], p + 1, 1), high)
+            left, right = sea[:, :LANES], sea[:, cols - LANES :]
+        low = jnp.where(lane == p, pltpu.roll(left, p, 1), low)
+        high = jnp.where(lane == p, pltpu.roll(right, p + 1, 1), high)
     down[...] = low
     up[...] = high
 
@@ -399,17 +421,25 @@
     )(*sources[2:], warm, salt)
     outer = lax.ppermute(outer, "grp", outer_pairs)
     blocks = home.shape[1]
-    planes, inner, own, down, up, sea, chosen = pl.pallas_call(
+    planes, inner, sea = pl.pallas_call(
         inner_kernel,
-        out_shape=[
-            near(NICE, rows, cols), message, tile, tile, tile, near(rows, cols), near(blocks * blocks, 8, LANES),
-        ],
-        in_specs=[vmem()] * 9 + [pl.BlockSpec(memory_space=pltpu.SMEM)],
-        out_specs=[vmem()] * 7,
+        out_shape=[near(NICE, rows, cols), message, near(rows, cols)],
+        in_specs=[anywhere] * len(sources),
+        out_specs=[vmem()] * 3,
+        scratch_shapes=[pltpu.VMEM(a.shape, a.dtype) for a in sources[2:]]
+        + [pltpu.SemaphoreType.DMA((2,)), pltpu.SemaphoreType.DMA((len(sources) - 2,))],
         name="inner_pack",
-    )(*sources, home)
+    )(*sources)
     inner = lax.ppermute(inner, "grp", inner_pairs)
-    up = lax.ppermute(up, "gy", up_pairs)
+    ends = [spec((levels, rows, LANES)), spec((levels, rows, LANES), (0, 0, cols // LANES - 1))]
+    own, down, up, chosen = pl.pallas_call(
+        tiles_kernel,
+        grid=(1,),
+        out_shape=[tile, tile, tile, near(blocks * blocks, 8, LANES)],
+        in_specs=ends * 2 + [vmem()] * 2 + [pl.BlockSpec(memory_space=pltpu.SMEM)],
+        out_specs=[vmem()] * 4,
+        name="tiles",
+    )(warm, warm, salt, salt, *held(planes, sea), home)
 
     edge, down = pl.pallas_call(
         edge_kernel,
@@ -419,6 +449,7 @@
         name="edge",
     )(*held(inner, outer, own, down))
     down = lax.ppermute(down, "gy", down_pairs)
+    up = lax.ppermute(up, "gy", up_pairs)
 
     velocity, picked = pl.pallas_call(
         ice_kernel,

time: 50.9 us -> 50.5 us (level)
  waiting for transfers between devices: 5.98 us -> 4.79 us
  Pallas kernels: 10.1 us -> 10.9 us
    pallas_call x0 -> x1, Pallas kernels: none -> 1.54 us  [per_device(): pl.pallas_call(tiles_kernel, grid=(1,), out_shape=[tile, tile, tile, near...]
    ppermute x1, waiting for transfers between devices: 0.98 us -> 0.12 us  [per_device(): outer = lax.ppermute(outer, 'grp', outer_pairs)]
    pallas_call x1, Pallas kernels: 2 us -> 1.31 us  [per_device(): pl.pallas_call(inner_kernel, out_shape=[near(NICE, rows, cols), message,...]
  transfers between devices with their start and end apart: 5 -> 5, of which waited for: 4 -> 3; matrix products, arithmetic and copies ran while one was open for 0% -> 0% of each run, Pallas kernels for 12% -> 14%
where the time goes in v4:
time: 50.5 us; the launch traced here: 50 us
  starting transfers between devices  33.6 us (67%)
  Pallas kernels  10.9 us (22%)
  waiting for transfers between devices  4.79 us (9%)
  between operations  0.7 us (1%)
    ppermute x1, starting transfers between devices, per_device(): outer = lax.ppermute(outer, 'grp', outer_pairs)  20.6 us
    all_to_all x1, starting transfers between devices, per_device(): lax.all_to_all(picked, 'gy', split_axis=0, concat_axis=0, tiled=True)  4.59 us
    pallas_call x1, Pallas kernels, per_device(): pl.pallas_call(tracer_kernel, grid=(steps,), in_specs=[vmem(), vmem(), vm...  4.23 us
    ppermute x1, starting transfers between devices, per_device(): up = lax.ppermute(up, 'gy', up_pairs)  3.36 us
    ppermute x1, starting transfers between devices, per_device(): down = lax.ppermute(down, 'gy', down_pairs)  3.17 us
    ppermute x1, waiting for transfers between devices, per_device(): down = lax.ppermute(down, 'gy', down_pairs)  2.5 us
    ppermute x1, waiting for transfers between devices, per_device(): up = lax.ppermute(up, 'gy', up_pairs)  2.16 us
    ppermute x1, starting transfers between devices, per_device(): inner = lax.ppermute(inner, 'grp', inner_pairs)  1.92 us
  transfers between devices with their start and end apart: 5, of which 3 were waited for; matrix products, arithmetic and copies ran while one was open for 0% of the time, Pallas kernels for 14%

profile of v4, /device:TPU:8, one launch (start us, length us, event | category | flops | bytes accessed | tf_op | source)
XLA Modules:
  0.0 50.0 jit_solution(14733144125006227742)
XLA Ops:
  0.6 1.1 %outer_pack.1 = f32[96,512]{1,0:T(8,128)S(1)} custom-call(f32[2,16,512]{2,1,0:T(8,128)} %refs_0_.3, f32[2,16,512]{2,1,0:T(8,128)} %refs_1_.3, f32[5,16,512]{2,1,0:T(8,128)} %refs_2_.3, f32[5,16,512]{2,1,0:T(8,128)} %cover.1, f32[5,16,512]{2,1,0:T(8,128)} %volume.1, s32[16,512]{1,0:T(8,128)} %refs_5_.3, s32[16,512]{1,0:T(8,128)} %icy.1, f32[24,16,512]{2,1,0:T(8,128)} %warm.1, ...), custom_call_target="tpu_custom_call" | custom-call | tf_op jit(solution)/shard_map/outer_pack/pallas_call | solution.py:413
  1.8 20.6 %collective-permute-start.2 = (f32[96,512]{1,0:T(8,128)S(1)}, f32[96,512]{1,0:T(8,128)S(1)}, u32[]{:S(2)}, u32[]{:S(2)}) collective-permute-start(f32[96,512]{1,0:T(8,128)S(1)} %outer_pack.1), channel_id=1, source_target_pairs={{4,8},{8,4},{12,16},{16,12},{20,24},{24,20},{28,32},{32,28},{36,40... | collective-permute-start | bytes 589832 | tf_op jit(solution)/shard_map/ppermute | solution.py:422
  22.4 1.3 %inner_pack.1 = (f32[12,16,512]{2,1,0:T(8,128)S(1)}, f32[96,512]{1,0:T(8,128)S(1)}, f32[16,512]{1,0:T(8,128)S(1)}) custom-call(f32[24,16,512]{2,1,0:T(8,128)} %warm.1, f32[24,16,512]{2,1,0:T(8,128)} %salt.1, f32[2,16,512]{2,1,0:T(8,128)} %refs_0_.3, f32[2,16,512]{2,1,0:T(8,128)} %refs_1_.3, f32[5,16,512]{2,1,0:T(8,128)} %refs_2_.3, f32[5,16,512]{2,1,0:T(8,128)} %cover.1, ...), custom_call_target="tpu_custom_call" | custom-call | tf_op jit(solution)/shard_map/inner_pack/pallas_call | solution.py:424
  23.7 1.9 %collective-permute-start.1 = (f32[96,512]{1,0:T(8,128)S(1)}, f32[96,512]{1,0:T(8,128)S(1)}, u32[]{:S(2)}, u32[]{:S(2)}) collective-permute-start(f32[96,512]{1,0:T(8,128)S(1)} %get-tuple-element.22), channel_id=1, source_target_pairs={{0,4},{4,0},{8,12},{12,8},{16,20},{20,16},{24,28},{28,24},{32,36},... | collective-permute-start | bytes 589832 | tf_op jit(solution)/shard_map/ppermute | solution.py:433
  25.6 1.5 %tiles.1 = (f32[16,128]{1,0:T(8,128)S(1)}, f32[16,128]{1,0:T(8,128)S(1)}, f32[16,128]{1,0:T(8,128)S(1)}, f32[16,8,128]{2,1,0:T(8,128)S(1)}) custom-call(f32[24,16,512]{2,1,0:T(8,128)} %warm.1, f32[24,16,512]{2,1,0:T(8,128)} %warm.1, f32[24,16,512]{2,1,0:T(8,128)} %salt.1, f32[24,16,512]{2,1,0:T(8,128)} %salt.1, f32[12,16,512]{2,1,0:T(8,128)S(1)} %get-tuple-element.20.planes, ...), custom_call_target="tpu_custom_call" | custom-call | tf_op jit(solution)/shard_map/tiles/pallas_call | solution.py:435
  27.2 0.1 collective-permute-done.2.outer
  27.3 0.0 collective-permute-done.1.inner
  27.3 0.1 edge.1
  27.4 3.2 %collective-permute-start.3 = (f32[40,128]{1,0:T(8,128)S(1)}, f32[40,128]{1,0:T(8,128)S(1)}, u32[]{:S(2)}, u32[]{:S(2)}) collective-permute-start(f32[40,128]{1,0:T(8,128)S(1)} %get-tuple-element.25), channel_id=1, source_target_pairs={{1,0},{2,1},{3,2},{5,4},{6,5},{7,6},{9,8},{10,9},{11,10},{13,12},{... | collective-permute-start | bytes 61448 | tf_op jit(solution)/shard_map/ppermute | solution.py:451
  30.6 2.5 %collective-permute-done.3.down = f32[40,128]{1,0:T(8,128)S(1)} collective-permute-done((f32[40,128]{1,0:T(8,128)S(1)}, f32[40,128]{1,0:T(8,128)S(1)}, u32[]{:S(2)}, u32[]{:S(2)}) %collective-permute-start.3) | collective-permute-done | bytes 20512 | tf_op jit(solution)/shard_map/ppermute | solution.py:451
  33.1 1.7 %ice.1 = (f32[2,16,512]{2,1,0:T(8,128)S(1)}, f32[4,6,16,128]{3,2,1,0:T(8,128)}) custom-call(f32[12,16,512]{2,1,0:T(8,128)S(1)} %get-tuple-element.20.planes, f32[12,8,512]{2,1,0:T(8,128)S(1)} %get-tuple-element.28.edge, f32[40,128]{1,0:T(8,128)S(1)} %collective-permute-done.3.down, f32[16,512]{1,0:T(8,128)S(1)} %get-tuple-element.19.sea.sea_in, ...), custom_call_target="tpu_custom_call" | custom-call | tf_op jit(solution)/shard_map/ice/pallas_call | solution.py:454
  34.9 4.6 %all-to-all-start = ((f32[4,6,16,128]{3,2,1,0:T(8,128)}), f32[4,6,16,128]{3,2,1,0:T(8,128)S(1)}, u32[]{:S(2)}, u32[]{:S(2)}) async-start(f32[4,6,16,128]{3,2,1,0:T(8,128)} %get-tuple-element.30), calls=%async_computation | async-start | bytes 393216 | tf_op jit(solution)/shard_map/all_to_all | solution.py:461
  39.4 3.4 %collective-permute-start = (f32[16,128]{1,0:T(8,128)S(1)}, f32[16,128]{1,0:T(8,128)S(1)}, u32[]{:S(2)}, u32[]{:S(2)}) collective-permute-start(f32[16,128]{1,0:T(8,128)S(1)} %get-tuple-element.21), channel_id=1, source_target_pairs={{0,1},{1,2},{2,3},{4,5},{5,6},{6,7},{8,9},{9,10},{10,11},{12,13},{... | collective-permute-start | bytes 24584 | tf_op jit(solution)/shard_map/ppermute | solution.py:452
  42.8 2.2 %collective-permute-done.up = f32[16,128]{1,0:T(8,128)S(1)} collective-permute-done((f32[16,128]{1,0:T(8,128)S(1)}, f32[16,128]{1,0:T(8,128)S(1)}, u32[]{:S(2)}, u32[]{:S(2)}) %collective-permute-start) | collective-permute-done | bytes 8224 | tf_op jit(solution)/shard_map/ppermute | solution.py:452
  45.0 4.2 %tracers.1 = (f32[24,16,512]{2,1,0:T(8,128)}, f32[24,16,512]{2,1,0:T(8,128)}) custom-call(f32[24,16,512]{2,1,0:T(8,128)} %warm.1, f32[24,16,512]{2,1,0:T(8,128)} %salt.1, f32[16,512]{1,0:T(8,128)S(1)} %get-tuple-element.19.sea.sea_in, s32[16,512]{1,0:T(8,128)} %icy.1, f32[5,16,512]{2,1,0:T(8,128)} %cover.1, f32[5,16,512]{2,1,0:T(8,128)} %volume.1, ...), custom_call_target="tpu_custom_call" | custom-call | tf_op jit(solution)/shard_map/tracers/pallas_call | solution.py:465
  49.2 0.0 all-to-all-done.owned
  49.2 0.8 %place.1 = (f32[5,16,512]{2,1,0:T(8,128)}, f32[2,16,512]{2,1,0:T(8,128)}) custom-call(f32[4,6,16,128]{3,2,1,0:T(8,128)S(1)} %all-to-all-done.owned, f32[2,16,512]{2,1,0:T(8,128)S(1)} %get-tuple-element.31.velocity, f32[16,512]{1,0:T(8,128)S(1)} %get-tuple-element.19.sea.sea_in), custom_call_target="tpu_custom_call" | custom-call | tf_op jit(solution)/shard_map/place/pallas_call | solution.py:484
Async XLA Ops:
  1.8 25.5 %collective-permute-start.2 = (f32[96,512]{1,0:T(8,128)S(1)}, f32[96,512]{1,0:T(8,128)S(1)}, u32[]{:S(2)}, u32[]{:S(2)}) collective-permute-start(f32[96,512]{1,0:T(8,128)S(1)} %outer_pack.1), channel_id=1, source_target_pairs={{4,8},{8,4},{12,16},{16,12},{20,24},{24,20},{28,32},{32,28},{36,40... | collective-permute-start | bytes 589832 | tf_op jit(solution)/shard_map/ppermute | solution.py:422
  23.7 3.6 %collective-permute-start.1 = (f32[96,512]{1,0:T(8,128)S(1)}, f32[96,512]{1,0:T(8,128)S(1)}, u32[]{:S(2)}, u32[]{:S(2)}) collective-permute-start(f32[96,512]{1,0:T(8,128)S(1)} %get-tuple-element.22), channel_id=1, source_target_pairs={{0,4},{4,0},{8,12},{12,8},{16,20},{20,16},{24,28},{28,24},{32,36},... | collective-permute-start | bytes 589832 | tf_op jit(solution)/shard_map/ppermute | solution.py:433
  27.4 5.7 %collective-permute-start.3 = (f32[40,128]{1,0:T(8,128)S(1)}, f32[40,128]{1,0:T(8,128)S(1)}, u32[]{:S(2)}, u32[]{:S(2)}) collective-permute-start(f32[40,128]{1,0:T(8,128)S(1)} %get-tuple-element.25), channel_id=1, source_target_pairs={{1,0},{2,1},{3,2},{5,4},{6,5},{7,6},{9,8},{10,9},{11,10},{13,12},{... | collective-permute-start | bytes 61448 | tf_op jit(solution)/shard_map/ppermute | solution.py:451
  34.9 14.4 %all-to-all-start = ((f32[4,6,16,128]{3,2,1,0:T(8,128)}), f32[4,6,16,128]{3,2,1,0:T(8,128)S(1)}, u32[]{:S(2)}, u32[]{:S(2)}) async-start(f32[4,6,16,128]{3,2,1,0:T(8,128)} %get-tuple-element.30), calls=%async_computation | async-start | bytes 393216 | tf_op jit(solution)/shard_map/all_to_all | solution.py:461
  39.4 5.5 %collective-permute-start = (f32[16,128]{1,0:T(8,128)S(1)}, f32[16,128]{1,0:T(8,128)S(1)}, u32[]{:S(2)}, u32[]{:S(2)}) collective-permute-start(f32[16,128]{1,0:T(8,128)S(1)} %get-tuple-element.21), channel_id=1, source_target_pairs={{0,1},{1,2},{2,3},{4,5},{5,6},{6,7},{8,9},{9,10},{10,11},{12,13},{... | collective-permute-start | bytes 24584 | tf_op jit(solution)/shard_map/ppermute | solution.py:452
